TPU v7x, 256 devices: a whole 4x4x8 slice. The times are simulated.
256 devices in a mesh: prow: 8 (over z_lo, y), pcol: 32 (over z_hi, x, core).
Axes of the slice: x: 4, y: 4, z: 8 (z_hi: 4, z_lo: 2; z = z_hi * 2 + z_lo), core: 2. Of those that a mesh axis runs over, the one named last changes fastest.
Arguments:
- ancestor_inverse: bfloat16 [24576, 24576], P('prow', 'pcol'), may hold values from -6 to 6
- tile_pattern: int32 [64, 64], replicated, may hold values 0 or 1
- rows_first: int32 [24576], replicated, may hold values 0 or 1
- rows_second: int32 [24576], replicated, may hold values 0 or 1
- panel_first: bfloat16 [24576, 512], P('prow', 'pcol'), may hold values from -0.0390625 to 0.0390625
- panel_second: bfloat16 [24576, 512], P('prow', 'pcol'), may hold values from -0.21875 to 0.21875
- inner_panel: bfloat16 [512, 512], replicated, may hold values from -0.25 to 0.25
- pivot_first: float32 [512, 512], replicated, may hold values from -6 to 6
- pivot_second: float32 [512, 512], replicated, may hold values from -6 to 6
Outputs:
- column_first: bfloat16 [24576, 512], P(('prow', 'pcol'))
- diagonal_first: float32 [512, 512], replicated
- inner_second: float32 [512, 512], replicated
- column_second: bfloat16 [24576, 512], P(('prow', 'pcol'))
- diagonal_second: float32 [512, 512], replicated
Inputs may be any that keep to these rules, and one draw needn't show every extreme that they name: `tile_pattern`: 1 marks a structurally nonzero tile. `rows_first`: 1 marks a row of the first supernode's structure. By construction here, a row belongs to the second supernode's structure only where both rows_second and rows_first are 1.
All inputs are finite; a program needn't handle non-finite values.
Results may differ from a plain program's by a relative error of at most 0.015.
Values may be sent and summed in bfloat16 or wider, within the bound.
A program may use at most 128 MiB of HBM per device.

v0:
```python
import jax
import jax.numpy as jnp
from jax import lax
from jax.sharding import PartitionSpec as P

TILE = 384


def from_root(shard, axis, root):
    mine = lax.axis_index(axis) == root
    return lax.psum(jnp.where(mine, shard, jnp.zeros_like(shard)), axis)


def mask_tiles(block, pattern, row_start, col_start):
    tile_rows = block.shape[0] // TILE
    tile_cols = block.shape[1] // TILE
    window = lax.dynamic_slice(pattern, (row_start, col_start), (tile_rows, tile_cols)).astype(
        jnp.bfloat16
    )
    shaped = block.reshape(tile_rows, TILE, tile_cols, TILE) * window[:, None, :, None]
    return shaped.reshape(block.shape)


def body(
    ancestor_inverse,
    tile_pattern,
    rows_first,
    rows_second,
    panel_first,
    panel_second,
    inner_panel,
    pivot_first,
    pivot_second,
):
    row_count = lax.axis_size("prow")
    col_count = lax.axis_size("pcol")
    row_id = lax.axis_index("prow")
    col_id = lax.axis_index("pcol")
    row_block = ancestor_inverse.shape[0]
    col_block = ancestor_inverse.shape[1]
    share = row_block // col_count
    sparse = mask_tiles(
        ancestor_inverse, tile_pattern, row_id * (row_block // TILE), col_id * (col_block // TILE)
    )
    struct_first = lax.dynamic_slice_in_dim(rows_first, row_id * row_block, row_block).astype(
        jnp.bfloat16
    )
    struct_second = struct_first * lax.dynamic_slice_in_dim(
        rows_second, row_id * row_block, row_block
    ).astype(jnp.bfloat16)
    local_first = panel_first * struct_first[:, None]
    local_second = panel_second * struct_second[:, None]
    source = col_id * row_count // col_count
    offset = col_id * col_block - source * row_block

    def summed_terms(columns):
        return jnp.dot(sparse, columns, preferred_element_type=jnp.float32)

    def ancestor_terms(local):
        full = lax.all_gather(local, "pcol", axis=1, tiled=True)
        mirrored = from_root(lax.dynamic_slice_in_dim(full, offset, col_block, 0), "prow", source)
        return (
            full,
            lax.psum_scatter(
                summed_terms(mirrored).astype(jnp.bfloat16), "pcol", scatter_dimension=0, tiled=True
            ).astype(jnp.float32),
        )

    full_first, sum_first = ancestor_terms(local_first)
    full_second, sum_second = ancestor_terms(local_second)
    column_first = (-sum_first).astype(jnp.bfloat16)
    own_first = lax.dynamic_slice_in_dim(full_first, col_id * share, share, 0)
    own_second = lax.dynamic_slice_in_dim(full_second, col_id * share, share, 0)
    corr_first, crossed = lax.psum(
        (
            jnp.dot(own_first.T, column_first, preferred_element_type=jnp.float32),
            jnp.dot(column_first.T, own_second, preferred_element_type=jnp.float32),
        ),
        ("prow", "pcol"),
    )
    diagonal_first = pivot_first - corr_first
    column_second = (
        -(sum_second + jnp.dot(column_first, inner_panel, preferred_element_type=jnp.float32))
    ).astype(jnp.bfloat16)
    inner_wide = inner_panel.astype(jnp.float32)
    inner_second = -(jnp.dot(diagonal_first, inner_wide, precision=lax.Precision.HIGHEST) + crossed)
    corr_second = lax.psum(
        jnp.dot(own_second.T, column_second, preferred_element_type=jnp.float32), ("prow", "pcol")
    )
    diagonal_second = (
        pivot_second
        - jnp.dot(inner_wide.T, inner_second, precision=lax.Precision.HIGHEST)
        - corr_second
    )
    return (column_first, diagonal_first, inner_second, column_second, diagonal_second)


def solution(mesh):
    return jax.shard_map(
        body,
        mesh=mesh,
        in_specs=(
            P("prow", "pcol"),
            P(),
            P(),
            P(),
            P("prow", "pcol"),
            P("prow", "pcol"),
            P(),
            P(),
            P(),
        ),
        out_specs=(P(("prow", "pcol"), None), P(), P(), P(("prow", "pcol"), None), P()),
        check_vma=False,
    )
```

profile of v0, /device:TPU:1, one launch (start us, length us, event | category | flops | bytes accessed | tf_op | source)
XLA Modules:
  0.0 700.5 jit_solution(2915164507721282915)
XLA Ops:
  7.2 0.0 all-gather.5.cloned.1.call-start
  7.2 0.8 fusion.13
  8.0 1.5 broadcast_multiply_fusion
  9.6 0.0 all-gather.3.cloned.1.call-start
  9.6 1.5 broadcast_multiply_fusion.1
  11.2 0.0 all-reduce.7.cloned.1.call-start
  11.3 61.1 %all-gather.5.cloned.1.call-done = bf16[3072,512]{0,1:T(8,128)(2,1)} async-done(((bf16[3072,16]{0,1:T(8,128)(2,1)}), bf16[3072,512]{0,1:T(8,128)(2,1)}) %all-gather.5.cloned.1.call-update) | async-done | bytes 3145744 | tf_op jit(solution)/shard_map/all_gather | solution.py:60
  72.4 2.1 dynamic-slice_select_fusion
  74.5 55.8 %all-gather.3.cloned.1.call-done = bf16[3072,512]{0,1:T(8,128)(2,1)} async-done(((bf16[3072,16]{0,1:T(8,128)(2,1)}), bf16[3072,512]{0,1:T(8,128)(2,1)}) %all-gather.3.cloned.1.call-update) | async-done | bytes 3145744 | tf_op jit(solution)/shard_map/all_gather | solution.py:60
  130.3 2.1 dynamic-slice_select_fusion.1
  132.5 0.0 reduce-scatter.3.cloned.1.call-start
  132.6 0.8 dynamic-slice_convert_fusion.2
  133.3 2.5 mul.55
  135.8 3.0 copy.18
  138.8 72.7 %all-reduce.7.cloned.1.call-done = (bf16[768,512]{0,1:T(8,128)(2,1)}, bf16[768,512]{0,1:T(8,128)(2,1)}) async-done(((bf16[768,512]{0,1:T(8,128)(2,1)}, bf16[768,512]{0,1:T(8,128)(2,1)}), (bf16[768,512]{0,1:T(8,128)(2,1)}, bf16[768,512]{0,1:T(8,128)(2,1)})) %all-reduce.7.cloned.1.call-update) | async-done | bytes 1572880 | tf_op jit(solution)/shard_map/psum | solution.py:11
  211.5 8.4 %convolution_convert_fusion.1 = bf16[3072,512]{1,0:T(8,128)(2,1)} fusion(bf16[768,512]{0,1:T(8,128)(2,1)} %get-tuple-element.13, bf16[3072,768]{1,0:T(8,128)(2,1)} %param.9, bf16[3072,768]{1,0:T(8,128)(2,1)} %bitcast.21), kind=kOutput, calls=%fused_computation.1 | convolution fusion | flops 2419851264 | bytes 13369344 | tf_op jit(solution)/shard_map/dot_general | solution.py:57
  219.9 0.0 reduce-scatter.5.cloned.1.call-start
  220.0 7.9 %convolution_convert_fusion = bf16[3072,512]{1,0:T(8,128)(2,1)} fusion(bf16[768,512]{0,1:T(8,128)(2,1)S(1)} %copy-done.9, bf16[3072,768]{1,0:T(8,128)(2,1)} %param.9, bf16[3072,768]{1,0:T(8,128)(2,1)} %bitcast.22), kind=kOutput, calls=%fused_computation | convolution fusion | flops 2419851264 | bytes 13369344 | tf_op jit(solution)/shard_map/dot_general | solution.py:57
  227.9 0.2 all-reduce.5.cloned.1.call-start
  228.1 89.8 %reduce-scatter.3.cloned.1.call-done = bf16[96,512]{1,0:T(8,128)(2,1)} async-done(((bf16[3072,512]{1,0:T(8,128)(2,1)}), bf16[96,512]{1,0:T(8,128)(2,1)}) %reduce-scatter.3.cloned.1.call-update) | async-done | bytes 98320 | tf_op jit(solution)/shard_map/reduce_scatter | solution.py:64
  317.9 0.9 negate_convert_fusion
  318.8 2.4 fusion.11
  321.2 2.3 fusion.7
  323.5 91.8 %reduce-scatter.5.cloned.1.call-done = bf16[96,512]{1,0:T(8,128)(2,1)} async-done(((bf16[3072,512]{1,0:T(8,128)(2,1)}), bf16[96,512]{1,0:T(8,128)(2,1)}) %reduce-scatter.5.cloned.1.call-update) | async-done | bytes 98320 | tf_op jit(solution)/shard_map/reduce_scatter | solution.py:64
  415.2 1.1 fusion.6
  416.4 2.4 fusion.9
  418.8 1.3 copy.14
  420.1 264.8 %all-reduce.5.cloned.1.call-done = (f32[512,512]{1,0:T(8,128)}, f32[512,512]{1,0:T(8,128)}, f32[512,512]{0,1:T(8,128)}) async-done(((f32[512,512]{1,0:T(8,128)}, f32[512,512]{1,0:T(8,128)}, f32[512,512]{0,1:T(8,128)}), (f32[512,512]{1,0:T(8,128)}, f32[512,512]{1,0:T(8,128)}, f32[512,512]{0,1:T(8,128)})) %all-reduce.5.cloned.1.call-update) | async-done | bytes 3145744 | tf_op jit(solution)/shard_map/psum | solution.py:74
  684.9 1.6 sub.18
  686.5 2.6 fusion.2
  689.1 2.0 fusion.4
  691.1 2.5 copy.16
  (26 shorter events, 0.2 us)
Async XLA Ops:
  7.2 408.1 %copy-start = (bf16[512,512]{1,0:T(8,128)(2,1)S(1)}, bf16[512,512]{1,0:T(8,128)(2,1)}, u32[]{:S(2)}) copy-start(bf16[512,512]{1,0:T(8,128)(2,1)} %param.15) | copy-start | bytes 1572868
  7.2 65.2 %all-gather.5.cloned.1.call-start = ((), (), s32[]{:S(2)}) async-start(), calls=%async_computation.4 | async-start | bytes 3244032 | tf_op jit(solution)/shard_map/all_gather | solution.py:60
  9.6 120.8 %all-gather.3.cloned.1.call-start = ((), (), s32[]{:S(2)}) async-start(), calls=%async_computation.2 | async-start | bytes 3244032 | tf_op jit(solution)/shard_map/all_gather | solution.py:60
  11.2 200.3 %all-reduce.7.cloned.1.call-start = ((), (), s32[]{:S(2)}) async-start(), calls=%async_computation.7 | async-start | bytes 3145728 | tf_op jit(solution)/shard_map/psum | solution.py:11
  132.5 185.4 %reduce-scatter.3.cloned.1.call-start = ((), (), s32[]{:S(2)}) async-start(), calls=%async_computation.3 | async-start | bytes 3244032 | tf_op jit(solution)/shard_map/reduce_scatter | solution.py:64
  211.5 8.4 %copy-start.9 = (bf16[768,512]{0,1:T(8,128)(2,1)S(1)}, bf16[768,512]{0,1:T(8,128)(2,1)}, u32[]{:S(2)}) copy-start(bf16[768,512]{0,1:T(8,128)(2,1)} %get-tuple-element.14) | copy-start | bytes 2359300
  219.9 195.3 %reduce-scatter.5.cloned.1.call-start = ((), (), s32[]{:S(2)}) async-start(), calls=%async_computation.5 | async-start | bytes 3244032 | tf_op jit(solution)/shard_map/reduce_scatter | solution.py:64
  227.9 190.9 %copy-start.6 = (f32[512,512]{1,0:T(8,128)S(1)}, f32[512,512]{1,0:T(8,128)}, u32[]{:S(2)}) copy-start(f32[512,512]{1,0:T(8,128)} %param.17) | copy-start | bytes 3145732
  227.9 457.0 %all-reduce.5.cloned.1.call-start = ((), (), s32[]{:S(2)}) async-start(), calls=%async_computation.6 | async-start | bytes 6291456 | tf_op jit(solution)/shard_map/psum | solution.py:74
  318.8 101.3 %copy-start.4 = (bf16[96,512]{1,0:T(8,128)(2,1)}, bf16[96,512]{1,0:T(8,128)(2,1)S(1)}, u32[]{:S(2)}) copy-start(bf16[96,512]{1,0:T(8,128)(2,1)S(1)} %negate_convert_fusion) | copy-start | bytes 294916
  318.8 366.1 %copy-start.5 = (f32[512,512]{1,0:T(8,128)S(1)}, f32[512,512]{1,0:T(8,128)}, u32[]{:S(2)}) copy-start(f32[512,512]{1,0:T(8,128)} %param.16) | copy-start | bytes 3145732
  416.3 270.1 %copy-start.8 = (bf16[96,512]{1,0:T(8,128)(2,1)}, bf16[96,512]{1,0:T(8,128)(2,1)S(1)}, u32[]{:S(2)}) copy-start(bf16[96,512]{1,0:T(8,128)(2,1)S(1)} %fusion.6) | copy-start | bytes 294916
  684.9 4.2 copy-start.3
  684.9 4.2 copy-start.7
  686.5 7.2 %copy-start.1 = (f32[512,512]{1,0:T(8,128)}, f32[512,512]{1,0:T(8,128)S(1)}, u32[]{:S(2)}) copy-start(f32[512,512]{1,0:T(8,128)S(1)} %sub.18) | copy-start | bytes 3145732
  689.1 4.6 copy-start.2
Sparse Core Ops, SparseCore 0:
  11.1 61.1 all-gather.4
  75.5 54.8 all-gather.2
  133.6 77.8 all-reduce.6
  220.0 97.7 reduce-scatter.2
  322.1 93.0 reduce-scatter.4
  421.4 263.3 all-reduce.4
where the time goes:
time: 702 us; the launch traced here: 701 us
  waiting for transfers between devices  636 us (91%)
  matrix products  29 us (4%)
  between operations  14.3 us (2%)
  other arithmetic  11.4 us (2%)
  local copies, waits for them, and re-layouts  9.39 us (1%)
    psum x1, waiting for transfers between devices, body(): lax.psum((jnp.dot(own_first.T, column_first, preferred_element_type=jnp.f...  265 us
    reduce_scatter x2, waiting for transfers between devices, ancestor_terms(): lax.psum_scatter(summed_terms(mirrored).astype(jnp.bfloat16), 'pcol', sca...  182 us
    all_gather x2, waiting for transfers between devices, ancestor_terms(): full = lax.all_gather(local, 'pcol', axis=1, tiled=True)  117 us
    psum x1, waiting for transfers between devices, from_root(): return lax.psum(jnp.where(mine, shard, jnp.zeros_like(shard)), axis)  72.7 us
    dot_general x2, matrix products, summed_terms(): return jnp.dot(sparse, columns, preferred_element_type=jnp.float32)  16.2 us
  transfers between devices with their start and end apart: 6, of which 6 were waited for; matrix products, arithmetic and copies ran while one was open for 4% of the time, Pallas kernels for 0%

commit v1 on v0

v1 whole, which is shorter than its diff:
```python
import jax
import jax.numpy as jnp
from jax import lax
from jax.experimental import pallas as pl
from jax.experimental.pallas import tpu as pltpu
from jax.sharding import PartitionSpec as P

TILE = 384
MESH = pl.DeviceIdType.MESH
BF16 = jnp.bfloat16
F32 = jnp.float32

NY, NX, NZH, NZL, NC = 4, 4, 4, 2, 2
BLOCK = 768
SHARE = 96
W = 512


def nt_dot(left, right):
    return lax.dot_general(left, right, (((1,), (1,)), ((), ())), preferred_element_type=F32)


def nn_dot(left, right):
    return jnp.dot(left, right, preferred_element_type=F32)


class Links:
    def __init__(self, send_sem, recv_sem):
        self.send_sem = send_sem
        self.recv_sem = recv_sem
        self.used = 0
        self.pending = []

    def slot(self):
        self.used += 1
        return self.used - 1

    def make(self, src, dst, device, slot):
        return pltpu.make_async_remote_copy(
            src_ref=src,
            dst_ref=dst,
            send_sem=self.send_sem.at[slot],
            recv_sem=self.recv_sem.at[slot],
            device_id=device,
            device_id_type=MESH,
        )

    def send(self, src, dst, device, slot=None, unless=None):
        slot = self.slot() if slot is None else slot
        copy = self.make(src, dst, device, slot)
        if unless is None:
            copy.start()
        else:
            pl.when(jnp.logical_not(unless))(copy.start)
        self.pending.append((copy, unless))
        return slot

    def arrived(self, ref, device, slot, unless=None):
        copy = self.make(ref, ref, device, slot)
        if unless is None:
            copy.wait_recv()
        else:
            pl.when(jnp.logical_not(unless))(copy.wait_recv)

    def drain(self):
        for copy, unless in self.pending:
            if unless is None:
                copy.wait_send()
            else:
                pl.when(jnp.logical_not(unless))(copy.wait_send)
        self.pending = []


def kernel(
    a_ref,
    keep_ref,
    xt_ref,
    inner_ref,
    c1_ref,
    c2_ref,
    xg,
    ao,
    ax,
    pt,
    ptx,
    mx,
    t,
    town,
    rxd,
    rx,
    s1,
    s1own,
    rzd,
    rz,
    g,
    ys,
    yown,
    ry,
    zsrc,
    zrecv,
    zg,
    send_sem,
    recv_sem,
    local_sem,
):
    r = lax.axis_index("prow")
    c = lax.axis_index("pcol")
    y = r % NY
    zl = r // NY
    zh = c // 8
    x = (c // 2) % NX
    core = c % 2
    j = c % 8
    z = zh * 2 + zl

    def at(yy=None, zz=None, xx=None, cc=None):
        yy = y if yy is None else yy
        zz = z if zz is None else zz
        xx = x if xx is None else xx
        cc = core if cc is None else cc
        return ((zz % 2) * NY + yy, (zz // 2) * 8 + xx * 2 + cc)

    mate = at(cc=1 - core)
    xn, xp = at(xx=(x + 1) % NX), at(xx=(x + 3) % NX)
    zhn, zhp = at(zz=(z + 2) % 8), at(zz=(z + 6) % 8)
    yn, yp = at(yy=(y + 1) % NY), at(yy=(y + 3) % NY)
    zmate = at(zz=zh * 2 + 1 - zl)
    y_peers = [at(yy=(y + d) % NY) for d in range(1, NY)]
    z_peers = [at(zz=(z + d) % 8) for d in range(1, 8)]

    local_a = pltpu.make_async_copy(a_ref.at[:, :, core], ao, local_sem.at[0])
    local_a.start()

    barrier = pltpu.get_barrier_semaphore()
    first_self = c // 4 == r
    own_self = 8 * (c // 8) + c // 4 == c
    for device in [mate, xn, xp] + y_peers + z_peers:
        pl.semaphore_signal(barrier, inc=1, device_id=device, device_id_type=MESH)
    for i in range(4):

        @pl.when(jnp.logical_not(first_self & (c % 4 == i)))
        def _():
            pl.semaphore_signal(barrier, inc=1, device_id=(c // 4, 4 * r + i), device_id_type=MESH)

        @pl.when(jnp.logical_not(own_self & (c % 4 == i)))
        def _():
            pl.semaphore_signal(barrier, inc=1, device_id=(r, 4 * j + i), device_id_type=MESH)

    pl.semaphore_wait(
        barrier, 13 + 8 - first_self.astype(jnp.int32) - own_self.astype(jnp.int32)
    )

    links = Links(send_sem, recv_sem)

    slice16 = pl.ds(pl.multiple_of(16 * (c % 4), 16), 16)
    first_slots = [links.slot() for _ in range(4)]
    own_slots = [links.slot() for _ in range(4)]

    def piece(q):
        return xt_ref.at[:, :, pl.ds(768 * q, 768)]

    base_first, base_own = first_slots[0], own_slots[0]
    for q in range(4):
        me = first_self & (c % 4 == q)
        copy = pltpu.make_async_remote_copy(
            src_ref=piece(q),
            dst_ref=pt.at[c // 4, :, slice16, :],
            send_sem=send_sem.at[base_first + q],
            recv_sem=recv_sem.at[base_first + c % 4],
            device_id=(c // 4, 4 * r + q),
            device_id_type=MESH,
        )
        pl.when(jnp.logical_not(me))(copy.start)
        links.pending.append((copy, me))

        @pl.when(me)
        def _():
            local = pltpu.make_async_copy(piece(q), pt.at[c // 4, :, slice16, :], local_sem.at[1])
            local.start()
            local.wait()

    a_slot = links.send(a_ref.at[:, :, 1 - core], ax, mate)

    for q in range(4):
        me = own_self & (c // 8 == q)
        copy = pltpu.make_async_remote_copy(
            src_ref=piece(q),
            dst_ref=mx.at[:, slice16, :],
            send_sem=send_sem.at[base_own + q],
            recv_sem=recv_sem.at[base_own + c % 4],
            device_id=(r, 8 * q + c // 4),
            device_id_type=MESH,
        )
        pl.when(jnp.logical_not(me))(copy.start)
        links.pending.append((copy, me))

        @pl.when(me)
        def _():
            local = pltpu.make_async_copy(piece(q), mx.at[:, slice16, :], local_sem.at[2])
            local.start()
            local.wait()

    for i in range(4):
        links.arrived(
            pt.at[r, :, pl.ds(16 * i, 16), :],
            mate,
            base_first + i,
            first_self & (c % 4 == i),
        )

    def row_of(yy, zz):
        return zz * NY + yy

    r_z = row_of(y, 1 - zl)
    got_z = links.send(pt.at[r], pt.at[r], zmate)
    got_yp = links.send(pt.at[r], pt.at[r], yn)
    got_yn = links.send(pt.at[r], pt.at[r], yp)
    f_own = links.send(pt.at[r], ptx.at[r], mate)

    def mask_chunk(i, _):
        m = i // NX
        n = i % NX
        ao[m, n] = (ao[m, n].astype(F32) * keep_ref[0, m, n]).astype(BF16)
        return 0

    local_a.wait()
    lax.fori_loop(0, NZH * NX, mask_chunk, 0)

    links.arrived(pt.at[r_z], zmate, got_z)
    got_yp_z = links.send(pt.at[r_z], pt.at[r_z], yn)
    got_yn_z = links.send(pt.at[r_z], pt.at[r_z], yp)
    f_z = links.send(pt.at[r_z], ptx.at[r_z], mate)

    ry_p, ry_n, ry_d = (y + 3) % NY, (y + 1) % NY, (y + 2) % NY
    forwarded = [(r, f_own), (r_z, f_z)]
    relayed = []
    for zz, slot_p, slot_n in ((zl, got_yp, got_yn), (1 - zl, got_yp_z, got_yn_z)):
        row_p, row_n, row_d = row_of(ry_p, zz), row_of(ry_n, zz), row_of(ry_d, zz)
        links.arrived(pt.at[row_p], yp, slot_p)
        got_d0 = links.send(pt.at[row_p, 0], pt.at[row_p, 0], yn)
        links.arrived(pt.at[row_n], yn, slot_n)
        got_d1 = links.send(pt.at[row_n, 1], pt.at[row_n, 1], yp)
        forwarded.append((row_p, links.send(pt.at[row_p], ptx.at[row_p], mate)))
        forwarded.append((row_n, links.send(pt.at[row_n], ptx.at[row_n], mate)))
        relayed.append((row_d, got_d0, got_d1))
    links.arrived(ax, mate, a_slot)

    def mask_other(i, _):
        m = i // NX
        n = i % NX
        ax[m, n] = (ax[m, n].astype(F32) * keep_ref[1, m, n]).astype(BF16)
        return 0

    lax.fori_loop(0, NZH * NX, mask_other, 0)
    for row_d, got_d0, got_d1 in relayed:
        links.arrived(pt.at[row_d, 0], yp, got_d0)
        links.arrived(pt.at[row_d, 1], yn, got_d1)
        forwarded.append((row_d, links.send(pt.at[row_d], ptx.at[row_d], mate)))
    for row, slot in forwarded:
        links.arrived(ptx.at[row], mate, slot)

    def product(p, xx, out):
        left = ao[:, xx].reshape(NZH * SHARE, BLOCK)
        left_x = ax[:, xx].reshape(NZH * SHARE, BLOCK)
        for h in range(2):
            right = pt[pl.ds(4 * h, 4), p].reshape(256, BLOCK)
            right_x = ptx[pl.ds(4 * h, 4), p].reshape(256, BLOCK)
            value = nt_dot(left, right) + nt_dot(left_x, right_x)
            out[..., pl.ds(256 * h, 256)] = value.reshape(NZH, SHARE, 256).astype(out.dtype)

    slots = []
    for p in range(2):
        product(p, (x + 2) % NX, t.at[p, 0])
        got_p = links.send(t.at[p, 0, pl.ds(0, 2)], rxd.at[p, 0], xn)
        got_n = links.send(t.at[p, 0, pl.ds(2, 2)], rxd.at[p, 1], xp)
        product(p, (x + 1) % NX, t.at[p, 1])
        pure_p = links.send(t.at[p, 1, pl.ds(2, 2)], rx.at[p, 0, pl.ds(2, 2)], xn)
        product(p, (x + 3) % NX, t.at[p, 2])
        pure_n = links.send(t.at[p, 2, pl.ds(0, 2)], rx.at[p, 1, pl.ds(0, 2)], xp)
        product(p, x, town.at[p])
        slots.append((got_p, got_n, pure_p, pure_n))

    sums = []
    for p in range(2):
        got_p, got_n, pure_p, pure_n = slots[p]
        links.arrived(rxd.at[p, 0], xp, got_p)
        t[p, 1, 0:2] = (t[p, 1, 0:2].astype(F32) + rxd[p, 0].astype(F32)).astype(BF16)
        sum_p = links.send(t.at[p, 1, pl.ds(0, 2)], rx.at[p, 0, pl.ds(0, 2)], xn)
        links.arrived(rxd.at[p, 1], xn, got_n)
        t[p, 2, 2:4] = (t[p, 2, 2:4].astype(F32) + rxd[p, 1].astype(F32)).astype(BF16)
        sum_n = links.send(t.at[p, 2, pl.ds(2, 2)], rx.at[p, 1, pl.ds(2, 2)], xp)
        sums.append((sum_p, sum_n))

    half = SHARE // 2
    lo, hi = pl.ds(0, half), pl.ds(half, half)
    zh_n, zh_p, zh_d = (zh + 1) % NZH, (zh + 3) % NZH, (zh + 2) % NZH
    z_slots = []
    for p in range(2):
        _, _, pure_p, pure_n = slots[p]
        sum_p, sum_n = sums[p]
        links.arrived(rx.at[p, 0, pl.ds(2, 2)], xp, pure_p)
        links.arrived(rx.at[p, 1, pl.ds(0, 2)], xn, pure_n)
        links.arrived(rx.at[p, 0, pl.ds(0, 2)], xp, sum_p)
        links.arrived(rx.at[p, 1, pl.ds(2, 2)], xn, sum_n)

        def total(k):
            return town[p, k] + rx[p, 0, k].astype(F32) + rx[p, 1, k].astype(F32)

        s1[p, 0] = total(zh_d).astype(BF16)
        got_p = links.send(s1.at[p, 0, lo], rzd.at[p, 0], zhn)
        got_n = links.send(s1.at[p, 0, hi], rzd.at[p, 1], zhp)
        s1[p, 1] = total(zh_n).astype(BF16)
        pure_p = links.send(s1.at[p, 1, hi], rz.at[p, 0, hi], zhn)
        s1[p, 2] = total(zh_p).astype(BF16)
        pure_n = links.send(s1.at[p, 2, lo], rz.at[p, 1, lo], zhp)
        s1own[p] = total(zh)
        z_slots.append((got_p, got_n, pure_p, pure_n))

    z_sums = []
    for p in range(2):
        got_p, got_n, pure_p, pure_n = z_slots[p]
        links.arrived(rzd.at[p, 0], zhp, got_p)
        s1[p, 1, lo] = (s1[p, 1, lo].astype(F32) + rzd[p, 0].astype(F32)).astype(BF16)
        sum_p = links.send(s1.at[p, 1, lo], rz.at[p, 0, lo], zhn)
        links.arrived(rzd.at[p, 1], zhn, got_n)
        s1[p, 2, hi] = (s1[p, 2, hi].astype(F32) + rzd[p, 1].astype(F32)).astype(BF16)
        sum_n = links.send(s1.at[p, 2, hi], rz.at[p, 1, hi], zhp)
        z_sums.append((sum_p, sum_n))

    jn, jp, jd = (j + 2) % 8, (j + 6) % 8, (j + 4) % 8

    def gather_start(buf, fst, snd):
        own_p = links.send(buf(j), buf(j), xn)
        own_n = links.send(buf(j), buf(j), xp)
        own_m = links.send(buf(j), buf(j), mate)
        return own_p, own_n, own_m

    def gather_finish(buf, part, begun):
        own_p, own_n, own_m = begun
        links.arrived(buf(jp), xp, own_p)
        d0 = links.send(part(jp, 0), part(jp, 0), xn)
        links.arrived(buf(jn), xn, own_n)
        d1 = links.send(part(jn, 1), part(jn, 1), xp)
        m_p = links.send(buf(jp), buf(jp), mate)
        m_n = links.send(buf(jn), buf(jn), mate)
        links.arrived(part(jd, 0), xp, d0)
        links.arrived(part(jd, 1), xn, d1)
        m_d = links.send(buf(jd), buf(jd), mate)
        other = 1 - 2 * core
        links.arrived(buf(j + other), mate, own_m)
        links.arrived(buf(jp + other), mate, m_p)
        links.arrived(buf(jn + other), mate, m_n)
        links.arrived(buf(jd + other), mate, m_d)

    begun = []
    for p in range(2):
        _, _, pure_p, pure_n = z_slots[p]
        sum_p, sum_n = z_sums[p]
        links.arrived(rz.at[p, 0, hi], zhp, pure_p)
        links.arrived(rz.at[p, 1, lo], zhn, pure_n)
        links.arrived(rz.at[p, 0, lo], zhp, sum_p)
        links.arrived(rz.at[p, 1, hi], zhn, sum_n)
        total_sum = s1own[p] + rz[p, 0].astype(F32) + rz[p, 1].astype(F32)
        if p == 0:
            column = (-total_sum).astype(BF16)
            c1_ref[...] = column
        else:
            column = (-(total_sum + nn_dot(c1_ref[...], inner_ref[...]))).astype(BF16)
            c2_ref[...] = column
        g[p, j] = column
        begun.append(gather_start(lambda k: g.at[p, k], None, None))
    for p in range(2):
        gather_finish(
            lambda k: g.at[p, k],
            lambda k, h: g.at[p, k, pl.ds(half * h, half)],
            begun[p],
        )

    for i in range(4):
        links.arrived(
            mx.at[:, pl.ds(16 * i, 16), :],
            mate,
            base_own + i,
            own_self & (c % 4 == i),
        )
    for k, (m, p) in enumerate(((0, 0), (1, 0), (1, 1))):
        rows = nn_dot(mx[m], g[p].reshape(BLOCK, W))
        for d in range(NY):
            part = rows[:, 128 * d : 128 * d + 128]
            ys[d, pl.ds(64 * k, 64)] = part.astype(BF16)
            yown[d, pl.ds(64 * k, 64)] = part

    y_slots = []
    for d in range(1, NY):
        y_slots.append(links.send(ys.at[(y + d) % NY], ry.at[d - 1], y_peers[d - 1]))
    total_y = yown[y]
    for d in range(1, NY):
        links.arrived(ry.at[d - 1], y_peers[d - 1], y_slots[d - 1])
        total_y = total_y + ry[d - 1].astype(F32)
    zsrc[...] = total_y.reshape(8, 24, 128)
    z_rs = []
    for d in range(1, 8):
        z_rs.append(links.send(zsrc.at[(z + d) % 8], zrecv.at[d - 1], z_peers[d - 1]))
    total_z = zsrc[z]
    for d in range(1, 8):
        links.arrived(zrecv.at[d - 1], z_peers[d - 1], z_rs[d - 1])
        total_z = total_z + zrecv[d - 1]
    zg[z] = total_z
    z_ag = []
    for d in range(1, 8):
        z_ag.append(links.send(zg.at[z], zg.at[z], z_peers[d - 1]))
    for d in range(1, 8):
        links.arrived(zg.at[(z + 8 - d) % 8], z_peers[d - 1], z_ag[d - 1])
    xg[j, y] = zg[...].reshape(192, 128).astype(BF16)
    y_ag = []
    for d in range(1, NY):
        y_ag.append(links.send(xg.at[j, y], xg.at[j, y], y_peers[d - 1]))
    for d in range(1, NY):
        links.arrived(xg.at[j, (y + NY - d) % NY], y_peers[d - 1], y_ag[d - 1])
    begun_x = gather_start(lambda k: xg.at[k], None, None)
    gather_finish(
        lambda k: xg.at[k], lambda k, h: xg.at[k, pl.ds(2 * h, 2)], begun_x
    )
    links.drain()


N_COPIES = 128


def body(
    ancestor_inverse,
    tile_pattern,
    rows_first,
    rows_second,
    panel_first,
    panel_second,
    inner_panel,
    pivot_first,
    pivot_second,
):
    row_id = lax.axis_index("prow")
    col_id = lax.axis_index("pcol")
    row_block, col_block = ancestor_inverse.shape
    struct_first = lax.dynamic_slice_in_dim(rows_first, row_id * row_block, row_block).astype(BF16)
    struct_second = struct_first * lax.dynamic_slice_in_dim(
        rows_second, row_id * row_block, row_block
    ).astype(BF16)
    local = jnp.stack([panel_first.T * struct_first[None, :], panel_second.T * struct_second[None, :]])

    window = lax.dynamic_slice(
        tile_pattern, (row_id * (row_block // TILE), (col_id // 2) * 4), (row_block // TILE, 4)
    ).astype(F32)
    core = col_id % 2
    own = lax.dynamic_slice_in_dim(window, 2 * core, 2, 1)
    other = lax.dynamic_slice_in_dim(window, 2 * (1 - core), 2, 1)
    keep = jnp.stack([own, other])
    keep = keep.reshape(2, NZH, 2, 1, 1, 2, 1)
    keep = jnp.broadcast_to(keep, (2, NZH, 2, 2, 1, 2, TILE)).reshape(2, NZH, NX, 1, col_block)

    halves = ancestor_inverse.reshape(NZH, NX, NC, SHARE, col_block)
    anywhere = pl.BlockSpec(memory_space=pl.ANY)
    vmem = pl.BlockSpec(memory_space=pltpu.VMEM)
    column_first, column_second, gathered = pl.pallas_call(
        kernel,
        out_shape=(
            jax.ShapeDtypeStruct((SHARE, W), BF16),
            jax.ShapeDtypeStruct((SHARE, W), BF16),
            jax.ShapeDtypeStruct((8, NY, 192, 128), BF16),
        ),
        in_specs=[anywhere, vmem, vmem, vmem],
        out_specs=(vmem, vmem, vmem),
        scratch_shapes=[
            pltpu.VMEM((NZH, NX, SHARE, BLOCK), BF16),
            pltpu.VMEM((NZH, NX, SHARE, BLOCK), BF16),
            pltpu.VMEM((8, 2, 64, BLOCK), BF16),
            pltpu.VMEM((8, 2, 64, BLOCK), BF16),
            pltpu.VMEM((2, 64, BLOCK), BF16),
            pltpu.VMEM((2, 3, NZH, SHARE, W), BF16),
            pltpu.VMEM((2, NZH, SHARE, W), F32),
            pltpu.VMEM((2, 2, 2, SHARE, W), BF16),
            pltpu.VMEM((2, 2, NZH, SHARE, W), BF16),
            pltpu.VMEM((2, 3, SHARE, W), BF16),
            pltpu.VMEM((2, SHARE, W), F32),
            pltpu.VMEM((2, 2, SHARE // 2, W), BF16),
            pltpu.VMEM((2, 2, SHARE, W), BF16),
            pltpu.VMEM((2, 8, SHARE, W), BF16),
            pltpu.VMEM((NY, 192, 128), BF16),
            pltpu.VMEM((NY, 192, 128), F32),
            pltpu.VMEM((NY - 1, 192, 128), BF16),
            pltpu.VMEM((8, 24, 128), F32),
            pltpu.VMEM((7, 24, 128), F32),
            pltpu.VMEM((8, 24, 128), F32),
            pltpu.SemaphoreType.DMA((N_COPIES,)),
            pltpu.SemaphoreType.DMA((N_COPIES,)),
            pltpu.SemaphoreType.DMA((3,)),
        ],
        compiler_params=pltpu.CompilerParams(
            collective_id=0, has_side_effects=True, vmem_limit_bytes=48 * 2**20
        ),
    )(halves, keep, local, inner_panel)

    products = gathered.reshape(8, NY, 3, 64, 128).transpose(2, 0, 3, 1, 4).reshape(3, W, W).astype(F32)
    corr_first, crossed_t, corr_second = products[0], products[1], products[2]
    diagonal_first = pivot_first - corr_first
    inner_wide = inner_panel.astype(F32)
    inner_second = -(
        jnp.dot(diagonal_first, inner_wide, precision=lax.Precision.HIGHEST) + crossed_t.T
    )
    diagonal_second = (
        pivot_second
        - jnp.dot(inner_wide.T, inner_second, precision=lax.Precision.HIGHEST)
        - corr_second
    )
    return (column_first, diagonal_first, inner_second, column_second, diagonal_second)


def solution(mesh):
    return jax.shard_map(
        body,
        mesh=mesh,
        in_specs=(
            P("prow", "pcol"),
            P(),
            P(),
            P(),
            P("prow", "pcol"),
            P("prow", "pcol"),
            P(),
            P(),
            P(),
        ),
        out_specs=(P(("prow", "pcol"), None), P(), P(), P(("prow", "pcol"), None), P()),
        check_vma=False,
    )
```

time: 702 us -> 156 us (0.22)
  waiting for transfers between devices: 636 us -> 0 us
  Pallas kernels: 0 us -> 132 us
  matrix products: 29 us -> 4.53 us
  between operations: 14.3 us -> 0.78 us
  other arithmetic: 11.4 us -> 4.33 us
    psum x2 -> x0, waiting for transfers between devices: 337 us -> none  [the longest x1 265 us: body(): lax.psum((jnp.dot(own_first.T, column_first, preferred_element_type=jnp.f...]
    reduce_scatter x2 -> x0, waiting for transfers between devices: 182 us -> none  [ancestor_terms(): lax.psum_scatter(summed_terms(mirrored).astype(jnp.bfloat16), 'pcol', sca...]
    pallas_call x0 -> x1, Pallas kernels: none -> 132 us  [body(): pl.pallas_call(kernel, out_shape=(jax.ShapeDtypeStruct((SHARE, W), BF16),...]
    all_gather x2 -> x0, waiting for transfers between devices: 117 us -> none  [ancestor_terms(): full = lax.all_gather(local, 'pcol', axis=1, tiled=True)]
    dot_general x6 -> x0, matrix products: 24.4 us -> none  [the longest x2 16.2 us: summed_terms(): return jnp.dot(sparse, columns, preferred_element_type=jnp.float32)]
  transfers between devices with their start and end apart: 6 -> 0, of which waited for: 6 -> 0; matrix products, arithmetic and copies ran while one was open for 4% -> 0% of each run, Pallas kernels for 0% -> 0%
where the time goes in v1:
time: 156 us
  Pallas kernels  132 us (85%)
  local copies, waits for them, and re-layouts  13.9 us (9%)
  matrix products  4.53 us (3%)
  other arithmetic  4.33 us (3%)
    pallas_call x1, Pallas kernels, body(): pl.pallas_call(kernel, out_shape=(jax.ShapeDtypeStruct((SHARE, W), BF16),...  132 us
    unnamed x16, local copies, waits for them, and re-layouts  7.29 us

profile of v1, /device:TPU:1, one launch (start us, length us, event | category | flops | bytes accessed | tf_op | source)
XLA Modules:
  0.0 155.5 jit_solution(11107751705547081030)
XLA Ops:
  0.7 0.8 dynamic-slice_convert_fusion.2
  1.4 0.1 constant_dynamic-slice_fusion.1
  1.5 0.1 copy.32
  1.6 0.1 copy.33
  1.7 0.1 copy.26
  1.9 0.1 broadcast_in_dim.12
  2.0 0.1 broadcast_in_dim.13.keep_ref
  2.1 0.7 fusion.3
  2.9 1.0 multiply_bitcast_fusion
  3.9 0.0 copy-start
  3.9 1.0 copy-done
  4.9 132.0 %shard_map.128 = (bf16[96,512]{1,0:T(8,128)(2,1)S(1)}, bf16[96,512]{1,0:T(8,128)(2,1)S(1)}, bf16[8,4,192,128]{3,2,1,0:T(8,128)(2,1)S(1)}) custom-call(bf16[4,4,2,96,768]{4,3,2,1,0:T(8,128)(2,1)} %bitcast.46, f32[2,4,4,1,768]{4,3,2,1,0:T(1,128)S(1)} %broadcast_in_dim.13.keep_ref, bf16[2,16,3072]{2,1,0:T(8,128)(2,1)S(1)} %pad_maximum_fusion.xt_ref, ...), custom_call_target="tpu_custom_call" | custom-call | tf_op jit(solution)/shard_map/pallas_call | solution.py:463
  136.9 1.5 copy.43
  138.4 1.6 %fusion.4 = (f32[1,8,64,4,128]{4,3,2,1,0:T(4,128)}, f32[1,8,64,4,128]{4,3,2,1,0:T(4,128)S(1)}, f32[1,8,64,4,128]{4,3,2,1,0:T(4,128)}) fusion(f32[3,8,64,4,128]{4,3,2,1,0:T(4,128)S(1)} %bitcast.45), kind=kLoop, calls=%fused_computation.19 | loop fusion | bytes 6291456 | tf_op jit(solution)/shard_map/slice | solution.py:503
  140.0 0.1 copy.45
  140.1 0.0 copy-start.1
  140.1 0.3 copy.28
  140.4 0.0 copy-start.4
  140.4 1.8 %bitcast_subtract_fusion = f32[512,512]{1,0:T(8,128)S(1)} fusion(f32[512,512]{1,0:T(8,128)} %param.16, f32[64,8,4,128]{3,2,1,0:T(4,128)} %bitcast.47), kind=kLoop, calls=%fused_computation.8 | loop fusion | flops 262144 | bytes 3145728 | tf_op jit(solution)/shard_map/sub | solution.py:504
  142.3 0.0 copy-done.1
  142.3 0.0 copy-start.2
  142.3 2.0 %fusion = f32[512,512]{1,0:T(8,128)} fusion(f32[512,512]{1,0:T(8,128)S(1)} %bitcast_subtract_fusion, bf16[512,512]{1,0:T(8,128)(2,1)S(1)} %copy-done.1, f32[512,512]{0,1:T(8,128)S(1)} %copy.28), kind=kOutput, calls=%fused_computation.2 | convolution fusion | flops 1611137024 | bytes 3670016 | tf_op jit(solution)/shard_map/dot_general | solution.py:507
  144.3 0.0 copy-done.4
  144.3 1.0 copy.44
  145.3 2.5 %copy.30 = f32[512,512]{0,1:T(8,128)} copy(f32[512,512]{1,0:T(8,128)} %bitcast.49) | data formatting | bytes 2097152 | tf_op jit(solution)/shard_map/squeeze | solution.py:503
  147.8 0.0 copy-done.2
  147.8 2.5 %copy.29 = f32[512,512]{0,1:T(8,128)} copy(f32[512,512]{1,0:T(8,128)} %param.17) | data formatting | bytes 2097152 | tf_op args[8]
  150.4 0.0 copy-done.3
  150.4 2.6 %fusion.2 = f32[512,512]{0,1:T(8,128)S(1)} fusion(f32[512,512]{0,1:T(8,128)} %copy.30, f32[512,512]{0,1:T(8,128)} %copy.29, f32[512,512]{1,0:T(8,128)S(1)} %copy-done.3, bf16[512,512]{1,0:T(8,128)(2,1)S(1)} %copy-done.1), kind=kOutput, calls=%fused_computation.5 | convolution fusion | flops 1611137024 | bytes 4718592 | tf_op jit(solution)/shard_map/dot_general | solution.py:511
  152.9 1.3 copy.31
  154.2 0.6 copy.48
  154.9 0.6 copy.49
  (3 shorter events, 0.0 us)
Async XLA Ops:
  3.9 1.0 copy-start
  140.1 2.2 %copy-start.1 = (bf16[512,512]{1,0:T(8,128)(2,1)S(1)}, bf16[512,512]{1,0:T(8,128)(2,1)}, u32[]{:S(2)}) copy-start(bf16[512,512]{1,0:T(8,128)(2,1)} %inner_ref.1) | copy-start | bytes 1572868
  140.4 3.8 %copy-start.4 = (f32[1,8,64,4,128]{4,3,2,1,0:T(4,128)S(1)}, f32[1,8,64,4,128]{4,3,2,1,0:T(4,128)}, u32[]{:S(2)}) copy-start(f32[1,8,64,4,128]{4,3,2,1,0:T(4,128)} %get-tuple-element.23) | copy-start | bytes 3145732
  142.3 5.5 %copy-start.2 = (f32[512,512]{1,0:T(8,128)}, f32[512,512]{1,0:T(8,128)S(1)}, u32[]{:S(2)}) copy-start(f32[512,512]{1,0:T(8,128)S(1)} %bitcast_subtract_fusion) | copy-start | bytes 3145732
  144.3 6.1 %copy-start.3 = (f32[512,512]{1,0:T(8,128)S(1)}, f32[512,512]{1,0:T(8,128)}, u32[]{:S(2)}) copy-start(f32[512,512]{1,0:T(8,128)} %fusion) | copy-start | bytes 3145732

commit v2 on v1

v2 whole, which is shorter than its diff:
```python
import jax
import jax.numpy as jnp
from jax import lax
from jax.experimental import pallas as pl
from jax.experimental.pallas import tpu as pltpu
from jax.sharding import PartitionSpec as P

TILE = 384
MESH = pl.DeviceIdType.MESH
BF16 = jnp.bfloat16
F32 = jnp.float32

NY, NX, NZH, NZL, NC = 4, 4, 4, 2, 2
BLOCK = 768
SHARE = 96
W = 512


def nt_dot(left, right):
    return lax.dot_general(left, right, (((1,), (1,)), ((), ())), preferred_element_type=F32)


def nn_dot(left, right):
    return jnp.dot(left, right, preferred_element_type=F32)


class Links:
    def __init__(self, send_sem, recv_sem):
        self.send_sem = send_sem
        self.recv_sem = recv_sem
        self.used = 0
        self.pending = []

    def slot(self):
        self.used += 1
        return self.used - 1

    def make(self, src, dst, device, slot):
        return pltpu.make_async_remote_copy(
            src_ref=src,
            dst_ref=dst,
            send_sem=self.send_sem.at[slot],
            recv_sem=self.recv_sem.at[slot],
            device_id=device,
            device_id_type=MESH,
        )

    def send(self, src, dst, device, slot=None, unless=None):
        slot = self.slot() if slot is None else slot
        copy = self.make(src, dst, device, slot)
        if unless is None:
            copy.start()
        else:
            pl.when(jnp.logical_not(unless))(copy.start)
        self.pending.append((copy, unless))
        return slot

    def arrived(self, ref, device, slot, unless=None):
        copy = self.make(ref, ref, device, slot)
        if unless is None:
            copy.wait_recv()
        else:
            pl.when(jnp.logical_not(unless))(copy.wait_recv)

    def drain(self):
        for copy, unless in self.pending:
            if unless is None:
                copy.wait_send()
            else:
                pl.when(jnp.logical_not(unless))(copy.wait_send)
        self.pending = []


def kernel(
    a_ref,
    pattern_ref,
    panel1_ref,
    panel2_ref,
    rows1_ref,
    rows2_ref,
    inner_ref,
    c1_ref,
    c2_ref,
    xg0,
    xg1,
    ao,
    ax,
    pattern,
    panels,
    rows,
    inner,
    xt,
    pt,
    ptx,
    mx,
    t,
    town,
    rxd,
    rx,
    s1,
    s1own,
    rzd,
    rz,
    g,
    ys,
    yown,
    ry,
    zsrc0,
    zrecv0,
    zg0,
    zsrc1,
    zrecv1,
    zg1,
    send_sem,
    recv_sem,
    local_sem,
):
    r = lax.axis_index("prow")
    c = lax.axis_index("pcol")
    y = r % NY
    zl = r // NY
    zh = c // 8
    x = (c // 2) % NX
    core = c % 2
    j = c % 8
    z = zh * 2 + zl

    def at(yy=None, zz=None, xx=None, cc=None):
        yy = y if yy is None else yy
        zz = z if zz is None else zz
        xx = x if xx is None else xx
        cc = core if cc is None else cc
        return ((zz % 2) * NY + yy, (zz // 2) * 8 + xx * 2 + cc)

    mate = at(cc=1 - core)
    xn, xp = at(xx=(x + 1) % NX), at(xx=(x + 3) % NX)
    zhn, zhp = at(zz=(z + 2) % 8), at(zz=(z + 6) % 8)
    yn, yp = at(yy=(y + 1) % NY), at(yy=(y + 3) % NY)
    zmate = at(zz=zh * 2 + 1 - zl)
    y_peers = [at(yy=(y + d) % NY) for d in range(1, NY)]
    z_peers = [at(zz=(z + d) % 8) for d in range(1, 8)]

    barrier = pltpu.get_barrier_semaphore()
    first_self = c // 4 == r
    own_self = 8 * (c // 8) + c // 4 == c
    for device in [mate, xn, xp] + y_peers + z_peers:
        pl.semaphore_signal(barrier, inc=1, device_id=device, device_id_type=MESH)
    for i in range(4):

        @pl.when(jnp.logical_not(first_self & (c % 4 == i)))
        def _():
            pl.semaphore_signal(barrier, inc=1, device_id=(c // 4, 4 * r + i), device_id_type=MESH)

        @pl.when(jnp.logical_not(own_self & (c % 4 == i)))
        def _():
            pl.semaphore_signal(barrier, inc=1, device_id=(r, 4 * j + i), device_id_type=MESH)

    own_rows = pl.ds(pl.multiple_of(24 * r, 8), 24)
    loads = [
        pltpu.make_async_copy(rows1_ref.at[own_rows], rows.at[0], local_sem.at[3]),
        pltpu.make_async_copy(rows2_ref.at[own_rows], rows.at[1], local_sem.at[4]),
        pltpu.make_async_copy(panel1_ref, panels.at[0], local_sem.at[5]),
        pltpu.make_async_copy(panel2_ref, panels.at[1], local_sem.at[6]),
        pltpu.make_async_copy(pattern_ref, pattern, local_sem.at[7]),
        pltpu.make_async_copy(a_ref.at[:, :, core], ao, local_sem.at[0]),
        pltpu.make_async_copy(inner_ref, inner, local_sem.at[8]),
    ]
    for load in loads:
        load.start()
    for load in loads[:4]:
        load.wait()
    keep1 = rows[0].astype(F32)
    keep2 = keep1 * rows[1].astype(F32)
    for p, keep in enumerate((keep1, keep2)):
        for k in range(24):
            cut = slice(128 * k, 128 * k + 128)
            xt[p, :, cut] = (panels[p, :, cut].astype(F32) * keep[k : k + 1]).astype(BF16)

    pl.semaphore_wait(
        barrier, 13 + 8 - first_self.astype(jnp.int32) - own_self.astype(jnp.int32)
    )

    links = Links(send_sem, recv_sem)

    slice16 = pl.ds(pl.multiple_of(16 * (c % 4), 16), 16)
    base_first = [links.slot() for _ in range(8)][0]
    base_own = [links.slot() for _ in range(4)][0]

    def spread(source, target, base, device, me, q, spare):
        copy = pltpu.make_async_remote_copy(
            src_ref=source,
            dst_ref=target,
            send_sem=send_sem.at[base + q],
            recv_sem=recv_sem.at[base + c % 4],
            device_id=device,
            device_id_type=MESH,
        )
        pl.when(jnp.logical_not(me))(copy.start)
        links.pending.append((copy, me))

        @pl.when(me)
        def _():
            local = pltpu.make_async_copy(source, target, local_sem.at[spare])
            local.start()
            local.wait()

    for p in range(2):
        for q in range(4):
            spread(
                xt.at[p, :, pl.ds(768 * q, 768)],
                pt.at[c // 4, p, slice16, :],
                base_first + 4 * p,
                (c // 4, 4 * r + q),
                first_self & (c % 4 == q),
                q,
                1,
            )

    a_slot = links.send(a_ref.at[:, :, 1 - core], ax, mate)

    for q in range(4):
        spread(
            xt.at[:, :, pl.ds(768 * q, 768)],
            mx.at[:, slice16, :],
            base_own,
            (r, 8 * q + c // 4),
            own_self & (c // 8 == q),
            q,
            2,
        )

    def mask_rows(ref, owner):
        def chunk(i, _):
            m = i // NX
            n = i % NX
            for k in range(2):
                cut = slice(TILE * k, TILE * k + TILE)
                keep = pattern[8 * r + 2 * m + n // 2, 2 * owner + k].astype(F32)
                ref[m, n, :, cut] = (ref[m, n, :, cut].astype(F32) * keep).astype(BF16)
            return 0

        lax.fori_loop(0, NZH * NX, chunk, 0)

    for load in loads[4:]:
        load.wait()
    mask_rows(ao, c)

    def row_of(yy, zz):
        return zz * NY + yy

    r_z = row_of(y, 1 - zl)
    y_p, y_n, y_d = (y + 3) % NY, (y + 1) % NY, (y + 2) % NY

    def panel_gather(p):
        forwarded = []

        def to(device, row):
            return links.send(pt.at[row, p], pt.at[row, p], device)

        def to_mate(row):
            forwarded.append((row, links.send(pt.at[row, p], ptx.at[row, p], mate)))

        def part(row, h):
            return pt.at[row, p, pl.ds(32 * h, 32)]

        for i in range(4):
            links.arrived(
                pt.at[r, p, pl.ds(16 * i, 16), :],
                mate,
                base_first + 4 * p + i,
                first_self & (c % 4 == i),
            )
        got_z, got_yp, got_yn = to(zmate, r), to(yn, r), to(yp, r)
        to_mate(r)
        yield
        links.arrived(pt.at[r_z, p], zmate, got_z)
        got_yp_z, got_yn_z = to(yn, r_z), to(yp, r_z)
        to_mate(r_z)
        yield
        relayed = []
        for zz, slot_p, slot_n in ((zl, got_yp, got_yn), (1 - zl, got_yp_z, got_yn_z)):
            row_p, row_n, row_d = row_of(y_p, zz), row_of(y_n, zz), row_of(y_d, zz)
            links.arrived(pt.at[row_p, p], yp, slot_p)
            got_d0 = links.send(part(row_p, 0), part(row_p, 0), yn)
            links.arrived(pt.at[row_n, p], yn, slot_n)
            got_d1 = links.send(part(row_n, 1), part(row_n, 1), yp)
            to_mate(row_p)
            to_mate(row_n)
            relayed.append((row_d, got_d0, got_d1))
            yield
        for row_d, got_d0, got_d1 in relayed:
            links.arrived(part(row_d, 0), yp, got_d0)
            links.arrived(part(row_d, 1), yn, got_d1)
            to_mate(row_d)
        yield
        for row, slot in forwarded:
            links.arrived(ptx.at[row, p], mate, slot)
        yield

    def product(p, xx, out):
        left = ao[:, xx].reshape(NZH * SHARE, BLOCK)
        left_x = ax[:, xx].reshape(NZH * SHARE, BLOCK)
        for h in range(2):
            right = pt[pl.ds(4 * h, 4), p].reshape(256, BLOCK)
            right_x = ptx[pl.ds(4 * h, 4), p].reshape(256, BLOCK)
            value = nt_dot(left, right) + nt_dot(left_x, right_x)
            out[..., pl.ds(256 * h, 256)] = value.reshape(NZH, SHARE, 256).astype(out.dtype)

    half = SHARE // 2
    lo, hi = pl.ds(0, half), pl.ds(half, half)
    zh_n, zh_p, zh_d = (zh + 1) % NZH, (zh + 3) % NZH, (zh + 2) % NZH
    jn, jp, jd = (j + 2) % 8, (j + 6) % 8, (j + 4) % 8

    def over_x_core(buf, part):
        own_p = links.send(buf(j), buf(j), xn)
        own_n = links.send(buf(j), buf(j), xp)
        own_m = links.send(buf(j), buf(j), mate)
        yield
        links.arrived(buf(jp), xp, own_p)
        d0 = links.send(part(jp, 0), part(jp, 0), xn)
        links.arrived(buf(jn), xn, own_n)
        d1 = links.send(part(jn, 1), part(jn, 1), xp)
        m_p = links.send(buf(jp), buf(jp), mate)
        m_n = links.send(buf(jn), buf(jn), mate)
        yield
        links.arrived(part(jd, 0), xp, d0)
        links.arrived(part(jd, 1), xn, d1)
        m_d = links.send(buf(jd), buf(jd), mate)
        yield
        other = 1 - 2 * core
        links.arrived(buf(j + other), mate, own_m)
        links.arrived(buf(jp + other), mate, m_p)
        links.arrived(buf(jn + other), mate, m_n)
        links.arrived(buf(jd + other), mate, m_d)

    def chain(p):
        product(p, (x + 2) % NX, t.at[p, 0])
        got_p = links.send(t.at[p, 0, pl.ds(0, 2)], rxd.at[p, 0], xn)
        got_n = links.send(t.at[p, 0, pl.ds(2, 2)], rxd.at[p, 1], xp)
        yield
        product(p, (x + 1) % NX, t.at[p, 1])
        pure_p = links.send(t.at[p, 1, pl.ds(2, 2)], rx.at[p, 0, pl.ds(2, 2)], xn)
        yield
        product(p, (x + 3) % NX, t.at[p, 2])
        pure_n = links.send(t.at[p, 2, pl.ds(0, 2)], rx.at[p, 1, pl.ds(0, 2)], xp)
        yield
        product(p, x, town.at[p])
        yield
        links.arrived(rxd.at[p, 0], xp, got_p)
        t[p, 1, 0:2] = (t[p, 1, 0:2].astype(F32) + rxd[p, 0].astype(F32)).astype(BF16)
        sum_p = links.send(t.at[p, 1, pl.ds(0, 2)], rx.at[p, 0, pl.ds(0, 2)], xn)
        links.arrived(rxd.at[p, 1], xn, got_n)
        t[p, 2, 2:4] = (t[p, 2, 2:4].astype(F32) + rxd[p, 1].astype(F32)).astype(BF16)
        sum_n = links.send(t.at[p, 2, pl.ds(2, 2)], rx.at[p, 1, pl.ds(2, 2)], xp)
        yield
        links.arrived(rx.at[p, 0, pl.ds(2, 2)], xp, pure_p)
        links.arrived(rx.at[p, 1, pl.ds(0, 2)], xn, pure_n)
        links.arrived(rx.at[p, 0, pl.ds(0, 2)], xp, sum_p)
        links.arrived(rx.at[p, 1, pl.ds(2, 2)], xn, sum_n)

        def total(k):
            return town[p, k] + rx[p, 0, k].astype(F32) + rx[p, 1, k].astype(F32)

        s1[p, 0] = total(zh_d).astype(BF16)
        got_p = links.send(s1.at[p, 0, lo], rzd.at[p, 0], zhn)
        got_n = links.send(s1.at[p, 0, hi], rzd.at[p, 1], zhp)
        s1[p, 1] = total(zh_n).astype(BF16)
        pure_p = links.send(s1.at[p, 1, hi], rz.at[p, 0, hi], zhn)
        s1[p, 2] = total(zh_p).astype(BF16)
        pure_n = links.send(s1.at[p, 2, lo], rz.at[p, 1, lo], zhp)
        s1own[p] = total(zh)
        yield
        links.arrived(rzd.at[p, 0], zhp, got_p)
        s1[p, 1, lo] = (s1[p, 1, lo].astype(F32) + rzd[p, 0].astype(F32)).astype(BF16)
        sum_p = links.send(s1.at[p, 1, lo], rz.at[p, 0, lo], zhn)
        links.arrived(rzd.at[p, 1], zhn, got_n)
        s1[p, 2, hi] = (s1[p, 2, hi].astype(F32) + rzd[p, 1].astype(F32)).astype(BF16)
        sum_n = links.send(s1.at[p, 2, hi], rz.at[p, 1, hi], zhp)
        yield
        links.arrived(rz.at[p, 0, hi], zhp, pure_p)
        links.arrived(rz.at[p, 1, lo], zhn, pure_n)
        links.arrived(rz.at[p, 0, lo], zhp, sum_p)
        links.arrived(rz.at[p, 1, hi], zhn, sum_n)
        total_sum = s1own[p] + rz[p, 0].astype(F32) + rz[p, 1].astype(F32)
        if p == 0:
            column = (-total_sum).astype(BF16)
            c1_ref[...] = column
        else:
            column = (-(total_sum + nn_dot(c1_ref[...], inner[...]))).astype(BF16)
            c2_ref[...] = column
        g[p, j] = column
        yield from over_x_core(
            lambda k: g.at[p, k], lambda k, h: g.at[p, k, pl.ds(half * h, half)]
        )

        if p == 0:
            for i in range(4):
                links.arrived(
                    mx.at[:, pl.ds(16 * i, 16), :],
                    mate,
                    base_own + i,
                    own_self & (c % 4 == i),
                )
        sides = (0, 1) if p == 0 else (1,)
        n = 64 * len(sides)
        xg, zsrc, zrecv, zg = ((xg0, zsrc0, zrecv0, zg0), (xg1, zsrc1, zrecv1, zg1))[p]
        for k, m in enumerate(sides):
            found = nn_dot(mx[m], g[p].reshape(BLOCK, W))
            for d in range(NY):
                part = found[:, 128 * d : 128 * d + 128]
                ys[p, d, pl.ds(64 * k, 64)] = part.astype(BF16)
                yown[p, d, pl.ds(64 * k, 64)] = part
        cut = pl.ds(0, n)
        y_rs = [
            links.send(ys.at[p, (y + d) % NY, cut], ry.at[p, d - 1, cut], y_peers[d - 1])
            for d in range(1, NY)
        ]
        yield
        total_y = yown[p, y, 0:n]
        for d in range(1, NY):
            links.arrived(ry.at[p, d - 1, cut], y_peers[d - 1], y_rs[d - 1])
            total_y = total_y + ry[p, d - 1, 0:n].astype(F32)
        zsrc[...] = total_y.reshape(8, n // 8, 128)
        z_rs = [
            links.send(zsrc.at[(z + d) % 8], zrecv.at[d - 1], z_peers[d - 1]) for d in range(1, 8)
        ]
        yield
        total_z = zsrc[z]
        for d in range(1, 8):
            links.arrived(zrecv.at[d - 1], z_peers[d - 1], z_rs[d - 1])
            total_z = total_z + zrecv[d - 1]
        zg[z] = total_z
        z_ag = [links.send(zg.at[z], zg.at[z], z_peers[d - 1]) for d in range(1, 8)]
        yield
        for d in range(1, 8):
            links.arrived(zg.at[(z + 8 - d) % 8], z_peers[d - 1], z_ag[d - 1])
        xg[j, y] = zg[...].reshape(n, 128).astype(BF16)
        y_ag = [links.send(xg.at[j, y], xg.at[j, y], y_peers[d - 1]) for d in range(1, NY)]
        yield
        for d in range(1, NY):
            links.arrived(xg.at[j, (y + NY - d) % NY], y_peers[d - 1], y_ag[d - 1])
        yield from over_x_core(lambda k: xg.at[k], lambda k, h: xg.at[k, pl.ds(2 * h, 2)])
        yield

    parts = {
        "f": panel_gather(0),
        "s": panel_gather(1),
        "A": chain(0),
        "B": chain(1),
    }
    for name in "ff" + "s" + "m" + "ff" + "s" + "f" + "s" + "f" + ORDER:
        if name == "m":
            links.arrived(ax, mate, a_slot)
            mask_rows(ax, c + 1 - 2 * core)
        else:
            next(parts[name])
    links.drain()


ORDER = "AsAsAAs" + "BABBBA" + "BAAABAABABABABABABABAB" + "BBBB"
N_COPIES = 160


def finish(
    inner_ref, pivot1_ref, pivot2_ref, xg0, xg1, d1_out, i2_out, d2_out, d1, i2, d2, crossed, sem
):
    def assemble(out, source, first, pivot):
        for k in range(8):
            for d in range(NY):
                rows, cols = slice(64 * k, 64 * k + 64), slice(128 * d, 128 * d + 128)
                part = source[k, d, first : first + 64].astype(F32)
                out[rows, cols] = part if pivot is None else pivot[rows, cols] - part

    def parts_dot(dot, wide):
        high = wide.astype(BF16)
        low = (wide - high.astype(F32)).astype(BF16)
        return dot(high) + dot(low)

    inner = inner_ref[...]
    assemble(d1, xg0, 0, pivot1_ref)
    copies = [pltpu.make_async_copy(d1, d1_out, sem.at[0])]
    copies[0].start()
    assemble(crossed, xg0, 64, None)
    i2[...] = -(parts_dot(lambda v: nn_dot(v, inner), d1[...]) + crossed[...].T)
    copies.append(pltpu.make_async_copy(i2, i2_out, sem.at[1]))
    copies[1].start()
    inner_t = inner.T
    assemble(d2, xg1, 0, pivot2_ref)
    d2[...] = d2[...] - parts_dot(lambda v: nn_dot(inner_t, v), i2[...])
    copies.append(pltpu.make_async_copy(d2, d2_out, sem.at[2]))
    copies[2].start()
    for copy in copies:
        copy.wait()


def body(
    ancestor_inverse,
    tile_pattern,
    rows_first,
    rows_second,
    panel_first,
    panel_second,
    inner_panel,
    pivot_first,
    pivot_second,
):
    col_block = ancestor_inverse.shape[1]
    halves = ancestor_inverse.reshape(NZH, NX, NC, SHARE, col_block)
    anywhere = pl.BlockSpec(memory_space=pl.ANY)
    vmem = pl.BlockSpec(memory_space=pltpu.VMEM)
    wide = jax.ShapeDtypeStruct((W, W), F32)
    column_first, column_second, gathered0, gathered1 = pl.pallas_call(
        kernel,
        out_shape=(
            jax.ShapeDtypeStruct((SHARE, W), BF16),
            jax.ShapeDtypeStruct((SHARE, W), BF16),
            jax.ShapeDtypeStruct((8, NY, 128, 128), BF16),
            jax.ShapeDtypeStruct((8, NY, 64, 128), BF16),
        ),
        in_specs=[anywhere] * 7,
        out_specs=(vmem, vmem, vmem, vmem),
        scratch_shapes=[
            pltpu.VMEM((NZH, NX, SHARE, BLOCK), BF16),
            pltpu.VMEM((NZH, NX, SHARE, BLOCK), BF16),
            pltpu.SMEM((64, 64), jnp.int32),
            pltpu.VMEM((2, 16, 3072), BF16),
            pltpu.VMEM((2, 24, 128), jnp.int32),
            pltpu.VMEM((W, W), BF16),
            pltpu.VMEM((2, 16, 3072), BF16),
            pltpu.VMEM((8, 2, 64, BLOCK), BF16),
            pltpu.VMEM((8, 2, 64, BLOCK), BF16),
            pltpu.VMEM((2, 64, BLOCK), BF16),
            pltpu.VMEM((2, 3, NZH, SHARE, W), BF16),
            pltpu.VMEM((2, NZH, SHARE, W), F32),
            pltpu.VMEM((2, 2, 2, SHARE, W), BF16),
            pltpu.VMEM((2, 2, NZH, SHARE, W), BF16),
            pltpu.VMEM((2, 3, SHARE, W), BF16),
            pltpu.VMEM((2, SHARE, W), F32),
            pltpu.VMEM((2, 2, SHARE // 2, W), BF16),
            pltpu.VMEM((2, 2, SHARE, W), BF16),
            pltpu.VMEM((2, 8, SHARE, W), BF16),
            pltpu.VMEM((2, NY, 128, 128), BF16),
            pltpu.VMEM((2, NY, 128, 128), F32),
            pltpu.VMEM((2, NY - 1, 128, 128), BF16),
            pltpu.VMEM((8, 16, 128), F32),
            pltpu.VMEM((7, 16, 128), F32),
            pltpu.VMEM((8, 16, 128), F32),
            pltpu.VMEM((8, 8, 128), F32),
            pltpu.VMEM((7, 8, 128), F32),
            pltpu.VMEM((8, 8, 128), F32),
            pltpu.SemaphoreType.DMA((N_COPIES,)),
            pltpu.SemaphoreType.DMA((N_COPIES,)),
            pltpu.SemaphoreType.DMA((9,)),
        ],
        compiler_params=pltpu.CompilerParams(
            collective_id=0, has_side_effects=True, vmem_limit_bytes=48 * 2**20
        ),
    )(
        halves,
        tile_pattern,
        panel_first.T,
        panel_second.T,
        rows_first.reshape(-1, 128),
        rows_second.reshape(-1, 128),
        inner_panel,
    )
    diagonal_first, inner_second, diagonal_second = pl.pallas_call(
        finish,
        out_shape=(wide, wide, wide),
        in_specs=[vmem] * 5,
        out_specs=(anywhere,) * 3,
        scratch_shapes=[pltpu.VMEM((W, W), F32)] * 4 + [pltpu.SemaphoreType.DMA((3,))],
        compiler_params=pltpu.CompilerParams(vmem_limit_bytes=32 * 2**20),
    )(inner_panel, pivot_first, pivot_second, gathered0, gathered1)
    return (column_first, diagonal_first, inner_second, column_second, diagonal_second)


def solution(mesh):
    return jax.shard_map(
        body,
        mesh=mesh,
        in_specs=(
            P("prow", "pcol"),
            P(),
            P(),
            P(),
            P("prow", "pcol"),
            P("prow", "pcol"),
            P(),
            P(),
            P(),
        ),
        out_specs=(P(("prow", "pcol"), None), P(), P(), P(("prow", "pcol"), None), P()),
        check_vma=False,
    )
```

time: 156 us -> 135 us (0.87)
  local copies, waits for them, and re-layouts: 13.9 us -> 6.65 us
  matrix products: 4.53 us -> 0 us
  other arithmetic: 4.33 us -> 0 us
  Pallas kernels: 132 us -> 128 us
    pallas_call x1, Pallas kernels: 132 us -> 125 us  [body(): pl.pallas_call(kernel, out_shape=(jax.ShapeDtypeStruct((SHARE, W), BF16),...]
    dot_general x2 -> x0, matrix products: 4.53 us -> none  [the longest x1 2.57 us: body(): jnp.dot(inner_wide.T, inner_second, precision=lax.Precision.HIGHEST)]
    squeeze x2 -> x0, local copies, waits for them, and re-layouts: 2.85 us -> none  [body(): corr_first, crossed_t, corr_second = (products[0], products[1], products[2])]
    pallas_call x0 -> x1, Pallas kernels: none -> 2.39 us  [body(): pl.pallas_call(finish, out_shape=(wide, wide, wide), in_specs=[vmem] * 5,...]
    sub x1 -> x0, other arithmetic: 1.84 us -> none  [body(): diagonal_first = pivot_first - corr_first]
    slice x1 -> x0, local copies, waits for them, and re-layouts: 1.62 us -> none  [body(): corr_first, crossed_t, corr_second = (products[0], products[1], products[2])]
    unnamed x16 -> x18, local copies, waits for them, and re-layouts: 7.29 us -> 6.65 us
where the time goes in v2:
time: 135 us
  Pallas kernels  128 us (95%)
  local copies, waits for them, and re-layouts  6.65 us (5%)
    pallas_call x1, Pallas kernels, body(): pl.pallas_call(kernel, out_shape=(jax.ShapeDtypeStruct((SHARE, W), BF16),...  125 us
    unnamed x18, local copies, waits for them, and re-layouts  6.65 us

profile of v2, /device:TPU:1, one launch (start us, length us, event | category | flops | bytes accessed | tf_op | source)
XLA Modules:
  0.0 135.1 jit_solution(15625622419673525273)
XLA Ops:
  0.6 0.0 copy-start
  0.6 1.0 copy-done
  1.7 0.0 copy-start.3
  1.7 0.9 copy-done.3
  2.6 0.0 copy-start.4
  2.6 0.9 copy-done.4
  3.5 0.0 copy-start.5
  3.5 0.9 copy-done.5
  4.4 0.0 copy-start.6
  4.4 0.9 copy-done.6
  5.2 0.0 copy-start.7
  5.3 0.8 copy-done.7
  6.0 0.0 copy-start.1
  6.0 0.0 copy-start.2
  6.0 125.4 %shard_map.128 = (bf16[96,512]{1,0:T(8,128)(2,1)S(1)}, bf16[96,512]{1,0:T(8,128)(2,1)S(1)}, bf16[8,4,128,128]{3,2,1,0:T(8,128)(2,1)S(1)}, bf16[8,4,64,128]{3,2,1,0:T(8,128)(2,1)S(1)}) custom-call(bf16[4,4,2,96,768]{4,3,2,1,0:T(8,128)(2,1)} %bitcast.9, s32[64,64]{1,0:T(8,128)S(1)} %copy-done.7, bf16[16,3072]{1,0:T(8,128)(2,1)S(1)} %bitcast.5, ...), custom_call_target="tpu_custom_call" | custom-call | tf_op jit(solution)/shard_map/pallas_call | solution.py:512
  131.4 0.0 copy-done.1
  131.4 0.0 copy-done.2
  131.4 2.4 %shard_map.129 = (f32[512,512]{1,0:T(8,128)}, f32[512,512]{1,0:T(8,128)}, f32[512,512]{1,0:T(8,128)}) custom-call(bf16[512,512]{1,0:T(8,128)(2,1)S(1)} %copy-done, f32[512,512]{1,0:T(8,128)S(1)} %copy-done.1, f32[512,512]{1,0:T(8,128)S(1)} %copy-done.2, bf16[8,4,128,128]{3,2,1,0:T(8,128)(2,1)S(1)} %get-tuple-element.13.xg0, ...), custom_call_target="tpu_custom_call" | custom-call | tf_op jit(solution)/shard_map/pallas_call | solution.py:567
  133.8 0.6 copy.16
  134.5 0.6 copy.17
Async XLA Ops:
  0.6 1.0 copy-start
  1.7 0.9 copy-start.3
  2.6 0.9 copy-start.4
  3.5 0.9 copy-start.5
  4.4 0.9 copy-start.6
  5.2 0.8 copy-start.7
  6.0 125.4 %copy-start.1 = (f32[512,512]{1,0:T(8,128)S(1)}, f32[512,512]{1,0:T(8,128)}, u32[]{:S(2)}) copy-start(f32[512,512]{1,0:T(8,128)} %pivot1_ref.1) | copy-start | bytes 3145732
  6.0 125.4 %copy-start.2 = (f32[512,512]{1,0:T(8,128)S(1)}, f32[512,512]{1,0:T(8,128)}, u32[]{:S(2)}) copy-start(f32[512,512]{1,0:T(8,128)} %pivot2_ref.1) | copy-start | bytes 3145732

commit v3 on v2

--- a/solution.py
+++ b/solution.py
@@ -102,15 +102,12 @@
     rzd,
     rz,
     g,
-    ys,
-    yown,
-    ry,
-    zsrc0,
-    zrecv0,
-    zg0,
-    zsrc1,
-    zrecv1,
-    zg1,
+    part0,
+    recv0,
+    back0,
+    part1,
+    recv1,
+    back1,
     send_sem,
     recv_sem,
     local_sem,
@@ -137,23 +134,34 @@
     zhn, zhp = at(zz=(z + 2) % 8), at(zz=(z + 6) % 8)
     yn, yp = at(yy=(y + 1) % NY), at(yy=(y + 3) % NY)
     zmate = at(zz=zh * 2 + 1 - zl)
-    y_peers = [at(yy=(y + d) % NY) for d in range(1, NY)]
-    z_peers = [at(zz=(z + d) % 8) for d in range(1, 8)]
+    diag_n, diag_p = at(yy=(y + 1) % NY, zz=zh * 2 + 1 - zl), at(yy=(y + 3) % NY, zz=zh * 2 + 1 - zl)
+
+    def yz_peer(e):
+        return (y + e // 8) % NY, (z + e % 8) % 8
 
     barrier = pltpu.get_barrier_semaphore()
     first_self = c // 4 == r
-    own_self = 8 * (c // 8) + c // 4 == c
-    for device in [mate, xn, xp] + y_peers + z_peers:
+    own_self = (c // 4 == r) & (8 * (c % 4) + r == c)
+    for device in [mate, xn, xp]:
         pl.semaphore_signal(barrier, inc=1, device_id=device, device_id_type=MESH)
+
+    def greet(e, _):
+        peer_y, peer_z = yz_peer(e)
+        pl.semaphore_signal(
+            barrier, inc=1, device_id=at(yy=peer_y, zz=peer_z), device_id_type=MESH
+        )
+        return 0
+
+    lax.fori_loop(1, 32, greet, 0)
     for i in range(4):
 
         @pl.when(jnp.logical_not(first_self & (c % 4 == i)))
         def _():
             pl.semaphore_signal(barrier, inc=1, device_id=(c // 4, 4 * r + i), device_id_type=MESH)
 
-        @pl.when(jnp.logical_not(own_self & (c % 4 == i)))
-        def _():
-            pl.semaphore_signal(barrier, inc=1, device_id=(r, 4 * j + i), device_id_type=MESH)
+    @pl.when(jnp.logical_not(own_self))
+    def _():
+        pl.semaphore_signal(barrier, inc=1, device_id=(j, 4 * r + zh), device_id_type=MESH)
 
     own_rows = pl.ds(pl.multiple_of(24 * r, 8), 24)
     loads = [
@@ -177,14 +185,14 @@
             xt[p, :, cut] = (panels[p, :, cut].astype(F32) * keep[k : k + 1]).astype(BF16)
 
     pl.semaphore_wait(
-        barrier, 13 + 8 - first_self.astype(jnp.int32) - own_self.astype(jnp.int32)
+        barrier, 34 + 5 - first_self.astype(jnp.int32) - own_self.astype(jnp.int32)
     )
 
     links = Links(send_sem, recv_sem)
 
     slice16 = pl.ds(pl.multiple_of(16 * (c % 4), 16), 16)
     base_first = [links.slot() for _ in range(8)][0]
-    base_own = [links.slot() for _ in range(4)][0]
+    own_slot = links.slot()
 
     def spread(source, target, base, device, me, q, spare):
         copy = pltpu.make_async_remote_copy(
@@ -218,16 +226,14 @@
 
     a_slot = links.send(a_ref.at[:, :, 1 - core], ax, mate)
 
-    for q in range(4):
-        spread(
-            xt.at[:, :, pl.ds(768 * q, 768)],
-            mx.at[:, slice16, :],
-            base_own,
-            (r, 8 * q + c // 4),
-            own_self & (c // 8 == q),
-            q,
-            2,
-        )
+    def send_own_rows():
+        links.send(pt.at[r], mx, (c // 4, 8 * (c % 4) + r), own_slot, own_self)
+
+        @pl.when(own_self)
+        def _():
+            local = pltpu.make_async_copy(pt.at[r], mx, local_sem.at[2])
+            local.start()
+            local.wait()
 
     def mask_rows(ref, owner):
         def chunk(i, _):
@@ -270,24 +276,25 @@
                 base_first + 4 * p + i,
                 first_self & (c % 4 == i),
             )
-        got_z, got_yp, got_yn = to(zmate, r), to(yn, r), to(yp, r)
+        got_yp, got_yn = to(yn, r), to(yp, r)
+        got_diag_p, got_diag_n = to(diag_n, r), to(diag_p, r)
+        got_z = to(zmate, r)
         to_mate(r)
         yield
-        links.arrived(pt.at[r_z, p], zmate, got_z)
-        got_yp_z, got_yn_z = to(yn, r_z), to(yp, r_z)
-        to_mate(r_z)
-        yield
         relayed = []
-        for zz, slot_p, slot_n in ((zl, got_yp, got_yn), (1 - zl, got_yp_z, got_yn_z)):
+        arrivals = ((zl, got_yp, got_yn, yp, yn), (1 - zl, got_diag_p, got_diag_n, diag_p, diag_n))
+        for zz, slot_p, slot_n, from_p, from_n in arrivals:
             row_p, row_n, row_d = row_of(y_p, zz), row_of(y_n, zz), row_of(y_d, zz)
-            links.arrived(pt.at[row_p, p], yp, slot_p)
+            links.arrived(pt.at[row_p, p], from_p, slot_p)
             got_d0 = links.send(part(row_p, 0), part(row_p, 0), yn)
-            links.arrived(pt.at[row_n, p], yn, slot_n)
+            links.arrived(pt.at[row_n, p], from_n, slot_n)
             got_d1 = links.send(part(row_n, 1), part(row_n, 1), yp)
             to_mate(row_p)
             to_mate(row_n)
             relayed.append((row_d, got_d0, got_d1))
-            yield
+        links.arrived(pt.at[r_z, p], zmate, got_z)
+        to_mate(r_z)
+        yield
         for row_d, got_d0, got_d1 in relayed:
             links.arrived(part(row_d, 0), yp, got_d0)
             links.arrived(part(row_d, 1), yn, got_d1)
@@ -344,14 +351,14 @@
         product(p, (x + 3) % NX, t.at[p, 2])
         pure_n = links.send(t.at[p, 2, pl.ds(0, 2)], rx.at[p, 1, pl.ds(0, 2)], xp)
         yield
-        product(p, x, town.at[p])
-        yield
         links.arrived(rxd.at[p, 0], xp, got_p)
         t[p, 1, 0:2] = (t[p, 1, 0:2].astype(F32) + rxd[p, 0].astype(F32)).astype(BF16)
         sum_p = links.send(t.at[p, 1, pl.ds(0, 2)], rx.at[p, 0, pl.ds(0, 2)], xn)
         links.arrived(rxd.at[p, 1], xn, got_n)
         t[p, 2, 2:4] = (t[p, 2, 2:4].astype(F32) + rxd[p, 1].astype(F32)).astype(BF16)
         sum_n = links.send(t.at[p, 2, pl.ds(2, 2)], rx.at[p, 1, pl.ds(2, 2)], xp)
+        yield
+        product(p, x, town.at[p])
         yield
         links.arrived(rx.at[p, 0, pl.ds(2, 2)], xp, pure_p)
         links.arrived(rx.at[p, 1, pl.ds(0, 2)], xn, pure_n)
@@ -394,51 +401,55 @@
         )
 
         if p == 0:
-            for i in range(4):
-                links.arrived(
-                    mx.at[:, pl.ds(16 * i, 16), :],
-                    mate,
-                    base_own + i,
-                    own_self & (c % 4 == i),
-                )
+            links.arrived(mx, mate, own_slot, own_self)
         sides = (0, 1) if p == 0 else (1,)
         n = 64 * len(sides)
-        xg, zsrc, zrecv, zg = ((xg0, zsrc0, zrecv0, zg0), (xg1, zsrc1, zrecv1, zg1))[p]
+        xg, part, recv, back = ((xg0, part0, recv0, back0), (xg1, part1, recv1, back1))[p]
         for k, m in enumerate(sides):
             found = nn_dot(mx[m], g[p].reshape(BLOCK, W))
             for d in range(NY):
-                part = found[:, 128 * d : 128 * d + 128]
-                ys[p, d, pl.ds(64 * k, 64)] = part.astype(BF16)
-                yown[p, d, pl.ds(64 * k, 64)] = part
-        cut = pl.ds(0, n)
-        y_rs = [
-            links.send(ys.at[p, (y + d) % NY, cut], ry.at[p, d - 1, cut], y_peers[d - 1])
-            for d in range(1, NY)
-        ]
-        yield
-        total_y = yown[p, y, 0:n]
-        for d in range(1, NY):
-            links.arrived(ry.at[p, d - 1, cut], y_peers[d - 1], y_rs[d - 1])
-            total_y = total_y + ry[p, d - 1, 0:n].astype(F32)
-        zsrc[...] = total_y.reshape(8, n // 8, 128)
-        z_rs = [
-            links.send(zsrc.at[(z + d) % 8], zrecv.at[d - 1], z_peers[d - 1]) for d in range(1, 8)
-        ]
-        yield
-        total_z = zsrc[z]
-        for d in range(1, 8):
-            links.arrived(zrecv.at[d - 1], z_peers[d - 1], z_rs[d - 1])
-            total_z = total_z + zrecv[d - 1]
-        zg[z] = total_z
-        z_ag = [links.send(zg.at[z], zg.at[z], z_peers[d - 1]) for d in range(1, 8)]
-        yield
-        for d in range(1, 8):
-            links.arrived(zg.at[(z + 8 - d) % 8], z_peers[d - 1], z_ag[d - 1])
-        xg[j, y] = zg[...].reshape(n, 128).astype(BF16)
-        y_ag = [links.send(xg.at[j, y], xg.at[j, y], y_peers[d - 1]) for d in range(1, NY)]
-        yield
-        for d in range(1, NY):
-            links.arrived(xg.at[j, (y + NY - d) % NY], y_peers[d - 1], y_ag[d - 1])
+                rows = found[:, 128 * d : 128 * d + 128]
+                step = n // 8
+                part[d, pl.ds(64 // step * k, 64 // step)] = rows.reshape(
+                    64 // step, step, 128
+                ).astype(part.dtype)
+        out_slot, back_slot = links.slot(), links.slot()
+
+        def to_all(copy_of):
+            def start(e, _):
+                copy_of(e).start()
+                return 0
+
+            lax.fori_loop(1, 32, start, 0)
+
+        def piece(e):
+            peer_y, peer_z = yz_peer(e)
+            return links.make(
+                part.at[peer_y, peer_z], recv.at[e - 1], at(yy=peer_y, zz=peer_z), out_slot
+            )
+
+        to_all(piece)
+        every = links.make(recv, recv, mate, out_slot)
+        links.pending.append((every, None))
+        yield
+        every.wait_recv()
+        total_yz = part[y, z].astype(F32)
+        for e in range(1, 32):
+            total_yz = total_yz + recv[e - 1].astype(F32)
+        back[y, z] = total_yz.astype(back.dtype)
+
+        def reply(e):
+            peer_y, peer_z = yz_peer(e)
+            return links.make(
+                back.at[y, z], back.at[y, z], at(yy=peer_y, zz=peer_z), back_slot
+            )
+
+        to_all(reply)
+        every = links.make(recv, recv, mate, back_slot)
+        links.pending.append((every, None))
+        yield
+        every.wait_recv()
+        xg[j] = back[...].reshape(NY, n, 128).astype(BF16)
         yield from over_x_core(lambda k: xg.at[k], lambda k, h: xg.at[k, pl.ds(2 * h, 2)])
         yield
 
@@ -448,21 +459,39 @@
         "A": chain(0),
         "B": chain(1),
     }
-    for name in "ff" + "s" + "m" + "ff" + "s" + "f" + "s" + "f" + ORDER:
+    for name in ORDER:
         if name == "m":
             links.arrived(ax, mate, a_slot)
             mask_rows(ax, c + 1 - 2 * core)
+        elif name == "o":
+            send_own_rows()
         else:
             next(parts[name])
     links.drain()
 
 
-ORDER = "AsAsAAs" + "BABBBA" + "BAAABAABABABABABABABAB" + "BBBB"
-N_COPIES = 160
+ORDER = "mfsoffsf" + "AsAAAsA" + "BBBA" + "BABAAB" + "AABBABBABABABABBB"
+N_COPIES = 128
 
 
 def finish(
-    inner_ref, pivot1_ref, pivot2_ref, xg0, xg1, d1_out, i2_out, d2_out, d1, i2, d2, crossed, sem
+        inner_ref,
+    pivot1_ref,
+    pivot2_ref,
+    xg0,
+    xg1,
+    c1_ref,
+    c2_ref,
+    d1_out,
+    i2_out,
+    d2_out,
+    c1_out,
+    c2_out,
+    d1,
+    i2,
+    d2,
+    crossed,
+    sem,
 ):
     def assemble(out, source, first, pivot):
         for k in range(8):
@@ -476,19 +505,25 @@
         low = (wide - high.astype(F32)).astype(BF16)
         return dot(high) + dot(low)
 
+    copies = [
+        pltpu.make_async_copy(c1_ref, c1_out, sem.at[3]),
+        pltpu.make_async_copy(c2_ref, c2_out, sem.at[4]),
+        pltpu.make_async_copy(d1, d1_out, sem.at[0]),
+        pltpu.make_async_copy(i2, i2_out, sem.at[1]),
+        pltpu.make_async_copy(d2, d2_out, sem.at[2]),
+    ]
+    copies[0].start()
+    copies[1].start()
     inner = inner_ref[...]
     assemble(d1, xg0, 0, pivot1_ref)
-    copies = [pltpu.make_async_copy(d1, d1_out, sem.at[0])]
-    copies[0].start()
+    copies[2].start()
     assemble(crossed, xg0, 64, None)
     i2[...] = -(parts_dot(lambda v: nn_dot(v, inner), d1[...]) + crossed[...].T)
-    copies.append(pltpu.make_async_copy(i2, i2_out, sem.at[1]))
-    copies[1].start()
+    copies[3].start()
     inner_t = inner.T
     assemble(d2, xg1, 0, pivot2_ref)
     d2[...] = d2[...] - parts_dot(lambda v: nn_dot(inner_t, v), i2[...])
-    copies.append(pltpu.make_async_copy(d2, d2_out, sem.at[2]))
-    copies[2].start()
+    copies[4].start()
     for copy in copies:
         copy.wait()
 
@@ -507,6 +542,7 @@
     col_block = ancestor_inverse.shape[1]
     halves = ancestor_inverse.reshape(NZH, NX, NC, SHARE, col_block)
     anywhere = pl.BlockSpec(memory_space=pl.ANY)
+    in_hbm = pl.BlockSpec(memory_space=pltpu.HBM)
     vmem = pl.BlockSpec(memory_space=pltpu.VMEM)
     wide = jax.ShapeDtypeStruct((W, W), F32)
     column_first, column_second, gathered0, gathered1 = pl.pallas_call(
@@ -517,7 +553,7 @@
             jax.ShapeDtypeStruct((8, NY, 128, 128), BF16),
             jax.ShapeDtypeStruct((8, NY, 64, 128), BF16),
         ),
-        in_specs=[anywhere] * 7,
+        in_specs=[in_hbm] * 7,
         out_specs=(vmem, vmem, vmem, vmem),
         scratch_shapes=[
             pltpu.VMEM((NZH, NX, SHARE, BLOCK), BF16),
@@ -539,15 +575,12 @@
             pltpu.VMEM((2, 2, SHARE // 2, W), BF16),
             pltpu.VMEM((2, 2, SHARE, W), BF16),
             pltpu.VMEM((2, 8, SHARE, W), BF16),
-            pltpu.VMEM((2, NY, 128, 128), BF16),
-            pltpu.VMEM((2, NY, 128, 128), F32),
-            pltpu.VMEM((2, NY - 1, 128, 128), BF16),
-            pltpu.VMEM((8, 16, 128), F32),
-            pltpu.VMEM((7, 16, 128), F32),
-            pltpu.VMEM((8, 16, 128), F32),
-            pltpu.VMEM((8, 8, 128), F32),
-            pltpu.VMEM((7, 8, 128), F32),
-            pltpu.VMEM((8, 8, 128), F32),
+            pltpu.VMEM((NY, 8, 16, 128), BF16),
+            pltpu.VMEM((31, 16, 128), BF16),
+            pltpu.VMEM((NY, 8, 16, 128), BF16),
+            pltpu.VMEM((NY, 8, 8, 128), F32),
+            pltpu.VMEM((31, 8, 128), F32),
+            pltpu.VMEM((NY, 8, 8, 128), F32),
             pltpu.SemaphoreType.DMA((N_COPIES,)),
             pltpu.SemaphoreType.DMA((N_COPIES,)),
             pltpu.SemaphoreType.DMA((9,)),
@@ -556,22 +589,30 @@
             collective_id=0, has_side_effects=True, vmem_limit_bytes=48 * 2**20
         ),
     )(
-        halves,
-        tile_pattern,
-        panel_first.T,
-        panel_second.T,
-        rows_first.reshape(-1, 128),
-        rows_second.reshape(-1, 128),
-        inner_panel,
+        *(
+            pltpu.with_memory_space_constraint(array, pltpu.HBM)
+            for array in (
+                halves,
+                tile_pattern,
+                panel_first.T,
+                panel_second.T,
+                rows_first.reshape(-1, 128),
+                rows_second.reshape(-1, 128),
+                inner_panel,
+            )
+        )
     )
-    diagonal_first, inner_second, diagonal_second = pl.pallas_call(
+    narrow = jax.ShapeDtypeStruct((SHARE, W), BF16)
+    diagonal_first, inner_second, diagonal_second, column_first, column_second = pl.pallas_call(
         finish,
-        out_shape=(wide, wide, wide),
-        in_specs=[vmem] * 5,
-        out_specs=(anywhere,) * 3,
-        scratch_shapes=[pltpu.VMEM((W, W), F32)] * 4 + [pltpu.SemaphoreType.DMA((3,))],
+        out_shape=(wide, wide, wide, narrow, narrow),
+        in_specs=[vmem] * 7,
+        out_specs=(anywhere,) * 5,
+        scratch_shapes=[pltpu.VMEM((W, W), F32)] * 4 + [pltpu.SemaphoreType.DMA((5,))],
         compiler_params=pltpu.CompilerParams(vmem_limit_bytes=32 * 2**20),
-    )(inner_panel, pivot_first, pivot_second, gathered0, gathered1)
+    )(
+        inner_panel, pivot_first, pivot_second, gathered0, gathered1, column_first, column_second
+    )
     return (column_first, diagonal_first, inner_second, column_second, diagonal_second)
 
 

time: 135 us -> 123 us (0.911)
  local copies, waits for them, and re-layouts: 6.65 us -> 0.01 us
  Pallas kernels: 128 us -> 122 us
    unnamed x18 -> x6, local copies, waits for them, and re-layouts: 6.65 us -> 0.01 us
    pallas_call x1, Pallas kernels: 125 us -> 119 us  [body(): pl.pallas_call(kernel, out_shape=(jax.ShapeDtypeStruct((SHARE, W), BF16),...]
where the time goes in v3:
time: 123 us
  Pallas kernels  122 us (99%)
    pallas_call x1, Pallas kernels, body(): pl.pallas_call(kernel, out_shape=(jax.ShapeDtypeStruct((SHARE, W), BF16),...  119 us
    pallas_call x1, Pallas kernels, body(): pl.pallas_call(finish, out_shape=(wide, wide, wide, narrow, narrow), in_s...  2.49 us

profile of v3, /device:TPU:1, one launch (start us, length us, event | category | flops | bytes accessed | tf_op | source)
XLA Modules:
  0.0 122.6 jit_solution(1382820895635648318)
XLA Ops:
  0.6 0.0 copy-start
  0.6 0.0 copy-start.2
  0.7 0.0 copy-start.1
  0.7 119.4 %shard_map.128 = (bf16[96,512]{1,0:T(8,128)(2,1)S(1)}, bf16[96,512]{1,0:T(8,128)(2,1)S(1)}, bf16[8,4,128,128]{3,2,1,0:T(8,128)(2,1)S(1)}, bf16[8,4,64,128]{3,2,1,0:T(8,128)(2,1)S(1)}) custom-call(bf16[4,4,2,96,768]{4,3,2,1,0:T(8,128)(2,1)} %bitcast.5, s32[64,64]{1,0:T(8,128)} %pattern_ref.1, bf16[16,3072]{1,0:T(8,128)(2,1)} %bitcast.6, ...), custom_call_target="tpu_custom_call" | custom-call | tf_op jit(solution)/shard_map/pallas_call | solution.py:548
  120.1 0.0 copy-done
  120.1 0.0 copy-done.2
  120.1 0.0 copy-done.1
  120.1 2.5 %shard_map.129 = (f32[512,512]{1,0:T(8,128)}, f32[512,512]{1,0:T(8,128)}, f32[512,512]{1,0:T(8,128)}, bf16[96,512]{1,0:T(8,128)(2,1)}, bf16[96,512]{1,0:T(8,128)(2,1)}) custom-call(bf16[512,512]{1,0:T(8,128)(2,1)S(1)} %copy-done, f32[512,512]{1,0:T(8,128)S(1)} %copy-done.1, f32[512,512]{1,0:T(8,128)S(1)} %copy-done.2, ...), custom_call_target="tpu_custom_call" | custom-call | tf_op jit(solution)/shard_map/pallas_call | solution.py:606
Async XLA Ops:
  0.6 119.5 %copy-start = (bf16[512,512]{1,0:T(8,128)(2,1)S(1)}, bf16[512,512]{1,0:T(8,128)(2,1)}, u32[]{:S(2)}) copy-start(bf16[512,512]{1,0:T(8,128)(2,1)} %inner_ref.3) | copy-start | bytes 1572868
  0.6 119.5 %copy-start.2 = (f32[512,512]{1,0:T(8,128)S(1)}, f32[512,512]{1,0:T(8,128)}, u32[]{:S(2)}) copy-start(f32[512,512]{1,0:T(8,128)} %pivot2_ref.1) | copy-start | bytes 3145732
  0.7 119.5 %copy-start.1 = (f32[512,512]{1,0:T(8,128)S(1)}, f32[512,512]{1,0:T(8,128)}, u32[]{:S(2)}) copy-start(f32[512,512]{1,0:T(8,128)} %pivot1_ref.1) | copy-start | bytes 3145732

commit v4 on v3

--- a/solution.py
+++ b/solution.py
@@ -134,8 +134,6 @@
     zhn, zhp = at(zz=(z + 2) % 8), at(zz=(z + 6) % 8)
     yn, yp = at(yy=(y + 1) % NY), at(yy=(y + 3) % NY)
     zmate = at(zz=zh * 2 + 1 - zl)
-    diag_n, diag_p = at(yy=(y + 1) % NY, zz=zh * 2 + 1 - zl), at(yy=(y + 3) % NY, zz=zh * 2 + 1 - zl)
-
     def yz_peer(e):
         return (y + e // 8) % NY, (z + e % 8) % 8
 
@@ -276,25 +274,24 @@
                 base_first + 4 * p + i,
                 first_self & (c % 4 == i),
             )
-        got_yp, got_yn = to(yn, r), to(yp, r)
-        got_diag_p, got_diag_n = to(diag_n, r), to(diag_p, r)
-        got_z = to(zmate, r)
+        got_z, got_yp, got_yn = to(zmate, r), to(yn, r), to(yp, r)
         to_mate(r)
         yield
+        links.arrived(pt.at[r_z, p], zmate, got_z)
+        got_yp_z, got_yn_z = to(yn, r_z), to(yp, r_z)
+        to_mate(r_z)
+        yield
         relayed = []
-        arrivals = ((zl, got_yp, got_yn, yp, yn), (1 - zl, got_diag_p, got_diag_n, diag_p, diag_n))
-        for zz, slot_p, slot_n, from_p, from_n in arrivals:
+        for zz, slot_p, slot_n in ((zl, got_yp, got_yn), (1 - zl, got_yp_z, got_yn_z)):
             row_p, row_n, row_d = row_of(y_p, zz), row_of(y_n, zz), row_of(y_d, zz)
-            links.arrived(pt.at[row_p, p], from_p, slot_p)
+            links.arrived(pt.at[row_p, p], yp, slot_p)
             got_d0 = links.send(part(row_p, 0), part(row_p, 0), yn)
-            links.arrived(pt.at[row_n, p], from_n, slot_n)
+            links.arrived(pt.at[row_n, p], yn, slot_n)
             got_d1 = links.send(part(row_n, 1), part(row_n, 1), yp)
             to_mate(row_p)
             to_mate(row_n)
             relayed.append((row_d, got_d0, got_d1))
-        links.arrived(pt.at[r_z, p], zmate, got_z)
-        to_mate(r_z)
-        yield
+            yield
         for row_d, got_d0, got_d1 in relayed:
             links.arrived(part(row_d, 0), yp, got_d0)
             links.arrived(part(row_d, 1), yn, got_d1)
@@ -470,7 +467,7 @@
     links.drain()
 
 
-ORDER = "mfsoffsf" + "AsAAAsA" + "BBBA" + "BABAAB" + "AABBABBABABABABBB"
+ORDER = "mffsffsfsf" + "AsAAsAsA" + "BBBA" + "BoABAAB" + "AABBABBABABABABBB"
 N_COPIES = 128
 
 

time: 123 us -> 128 us (1.041)
  Pallas kernels: 122 us -> 127 us
    pallas_call x1, Pallas kernels: 119 us -> 124 us  [body(): pl.pallas_call(kernel, out_shape=(jax.ShapeDtypeStruct((SHARE, W), BF16),...]
where the time goes in v4:
time: 128 us; the launch traced here: 127 us
  Pallas kernels  127 us (99%)
    pallas_call x1, Pallas kernels, body(): pl.pallas_call(kernel, out_shape=(jax.ShapeDtypeStruct((SHARE, W), BF16),...  124 us

profile of v4, /device:TPU:1, one launch (start us, length us, event | category | flops | bytes accessed | tf_op | source)
XLA Modules:
  0.0 127.5 jit_solution(2433704753682870069)
XLA Ops:
  0.6 0.0 copy-start
  0.6 0.0 copy-start.2
  0.7 0.0 copy-start.1
  0.7 124.3 %shard_map.128 = (bf16[96,512]{1,0:T(8,128)(2,1)S(1)}, bf16[96,512]{1,0:T(8,128)(2,1)S(1)}, bf16[8,4,128,128]{3,2,1,0:T(8,128)(2,1)S(1)}, bf16[8,4,64,128]{3,2,1,0:T(8,128)(2,1)S(1)}) custom-call(bf16[4,4,2,96,768]{4,3,2,1,0:T(8,128)(2,1)} %bitcast.5, s32[64,64]{1,0:T(8,128)} %pattern_ref.1, bf16[16,3072]{1,0:T(8,128)(2,1)} %bitcast.6, ...), custom_call_target="tpu_custom_call" | custom-call | tf_op jit(solution)/shard_map/pallas_call | solution.py:545
  125.0 0.0 copy-done
  125.0 0.0 copy-done.2
  125.0 0.0 copy-done.1
  125.0 2.5 %shard_map.129 = (f32[512,512]{1,0:T(8,128)}, f32[512,512]{1,0:T(8,128)}, f32[512,512]{1,0:T(8,128)}, bf16[96,512]{1,0:T(8,128)(2,1)}, bf16[96,512]{1,0:T(8,128)(2,1)}) custom-call(bf16[512,512]{1,0:T(8,128)(2,1)S(1)} %copy-done, f32[512,512]{1,0:T(8,128)S(1)} %copy-done.1, f32[512,512]{1,0:T(8,128)S(1)} %copy-done.2, ...), custom_call_target="tpu_custom_call" | custom-call | tf_op jit(solution)/shard_map/pallas_call | solution.py:603
Async XLA Ops:
  0.6 124.3 %copy-start = (bf16[512,512]{1,0:T(8,128)(2,1)S(1)}, bf16[512,512]{1,0:T(8,128)(2,1)}, u32[]{:S(2)}) copy-start(bf16[512,512]{1,0:T(8,128)(2,1)} %inner_ref.3) | copy-start | bytes 1572868
  0.6 124.3 %copy-start.2 = (f32[512,512]{1,0:T(8,128)S(1)}, f32[512,512]{1,0:T(8,128)}, u32[]{:S(2)}) copy-start(f32[512,512]{1,0:T(8,128)} %pivot2_ref.1) | copy-start | bytes 3145732
  0.7 124.3 %copy-start.1 = (f32[512,512]{1,0:T(8,128)S(1)}, f32[512,512]{1,0:T(8,128)}, u32[]{:S(2)}) copy-start(f32[512,512]{1,0:T(8,128)} %pivot1_ref.1) | copy-start | bytes 3145732

commit v5 on v4

--- a/solution.py
+++ b/solution.py
@@ -210,7 +210,7 @@
             local.start()
             local.wait()
 
-    for p in range(2):
+    def spread_panel(p):
         for q in range(4):
             spread(
                 xt.at[p, :, pl.ds(768 * q, 768)],
@@ -221,6 +221,8 @@
                 q,
                 1,
             )
+
+    spread_panel(0)
 
     a_slot = links.send(a_ref.at[:, :, 1 - core], ax, mate)
 
@@ -462,12 +464,14 @@
             mask_rows(ax, c + 1 - 2 * core)
         elif name == "o":
             send_own_rows()
+        elif name == "t":
+            spread_panel(1)
         else:
             next(parts[name])
     links.drain()
 
 
-ORDER = "mffsffsfsf" + "AsAAsAsA" + "BBBA" + "BoABAAB" + "AABBABBABABABABBB"
+ORDER = "mftffsofsffAsAAsAsAsBBBABABAABAABBBABBABABABABB"
 N_COPIES = 128
 
 

time: 128 us -> 120 us (0.938)
  Pallas kernels: 127 us -> 119 us
    pallas_call x1, Pallas kernels: 124 us -> 116 us  [body(): pl.pallas_call(kernel, out_shape=(jax.ShapeDtypeStruct((SHARE, W), BF16),...]
where the time goes in v5:
time: 120 us
  Pallas kernels  119 us (99%)
    pallas_call x1, Pallas kernels, body(): pl.pallas_call(kernel, out_shape=(jax.ShapeDtypeStruct((SHARE, W), BF16),...  116 us
    pallas_call x1, Pallas kernels, body(): pl.pallas_call(finish, out_shape=(wide, wide, wide, narrow, narrow), in_s...  2.5 us

profile of v5, /device:TPU:1, one launch (start us, length us, event | category | flops | bytes accessed | tf_op | source)
XLA Modules:
  0.0 119.6 jit_solution(17514965223448502882)
XLA Ops:
  0.6 0.0 copy-start
  0.6 0.0 copy-start.2
  0.7 0.0 copy-start.1
  0.7 116.4 %shard_map.128 = (bf16[96,512]{1,0:T(8,128)(2,1)S(1)}, bf16[96,512]{1,0:T(8,128)(2,1)S(1)}, bf16[8,4,128,128]{3,2,1,0:T(8,128)(2,1)S(1)}, bf16[8,4,64,128]{3,2,1,0:T(8,128)(2,1)S(1)}) custom-call(bf16[4,4,2,96,768]{4,3,2,1,0:T(8,128)(2,1)} %bitcast.5, s32[64,64]{1,0:T(8,128)} %pattern_ref.1, bf16[16,3072]{1,0:T(8,128)(2,1)} %bitcast.6, ...), custom_call_target="tpu_custom_call" | custom-call | tf_op jit(solution)/shard_map/pallas_call | solution.py:549
  117.0 0.0 copy-done
  117.0 0.0 copy-done.2
  117.1 0.0 copy-done.1
  117.1 2.5 %shard_map.129 = (f32[512,512]{1,0:T(8,128)}, f32[512,512]{1,0:T(8,128)}, f32[512,512]{1,0:T(8,128)}, bf16[96,512]{1,0:T(8,128)(2,1)}, bf16[96,512]{1,0:T(8,128)(2,1)}) custom-call(bf16[512,512]{1,0:T(8,128)(2,1)S(1)} %copy-done, f32[512,512]{1,0:T(8,128)S(1)} %copy-done.1, f32[512,512]{1,0:T(8,128)S(1)} %copy-done.2, ...), custom_call_target="tpu_custom_call" | custom-call | tf_op jit(solution)/shard_map/pallas_call | solution.py:607
Async XLA Ops:
  0.6 116.4 %copy-start = (bf16[512,512]{1,0:T(8,128)(2,1)S(1)}, bf16[512,512]{1,0:T(8,128)(2,1)}, u32[]{:S(2)}) copy-start(bf16[512,512]{1,0:T(8,128)(2,1)} %inner_ref.3) | copy-start | bytes 1572868
  0.6 116.4 %copy-start.2 = (f32[512,512]{1,0:T(8,128)S(1)}, f32[512,512]{1,0:T(8,128)}, u32[]{:S(2)}) copy-start(f32[512,512]{1,0:T(8,128)} %pivot2_ref.1) | copy-start | bytes 3145732
  0.7 116.4 %copy-start.1 = (f32[512,512]{1,0:T(8,128)S(1)}, f32[512,512]{1,0:T(8,128)}, u32[]{:S(2)}) copy-start(f32[512,512]{1,0:T(8,128)} %pivot1_ref.1) | copy-start | bytes 3145732

commit v6 on v5

--- a/solution.py
+++ b/solution.py
@@ -138,7 +138,7 @@
         return (y + e // 8) % NY, (z + e % 8) % 8
 
     barrier = pltpu.get_barrier_semaphore()
-    first_self = c // 4 == r
+    first_self = (c // 4 == r) & (j == r)
     own_self = (c // 4 == r) & (8 * (c % 4) + r == c)
     for device in [mate, xn, xp]:
         pl.semaphore_signal(barrier, inc=1, device_id=device, device_id_type=MESH)
@@ -153,9 +153,9 @@
     lax.fori_loop(1, 32, greet, 0)
     for i in range(4):
 
-        @pl.when(jnp.logical_not(first_self & (c % 4 == i)))
+        @pl.when(jnp.logical_not(first_self & (zh == i)))
         def _():
-            pl.semaphore_signal(barrier, inc=1, device_id=(c // 4, 4 * r + i), device_id_type=MESH)
+            pl.semaphore_signal(barrier, inc=1, device_id=(c // 4, 8 * i + r), device_id_type=MESH)
 
     @pl.when(jnp.logical_not(own_self))
     def _():
@@ -188,7 +188,7 @@
 
     links = Links(send_sem, recv_sem)
 
-    slice16 = pl.ds(pl.multiple_of(16 * (c % 4), 16), 16)
+    slice16 = pl.ds(pl.multiple_of(16 * zh, 16), 16)
     base_first = [links.slot() for _ in range(8)][0]
     own_slot = links.slot()
 
@@ -197,7 +197,7 @@
             src_ref=source,
             dst_ref=target,
             send_sem=send_sem.at[base + q],
-            recv_sem=recv_sem.at[base + c % 4],
+            recv_sem=recv_sem.at[base + zh],
             device_id=device,
             device_id_type=MESH,
         )
@@ -214,9 +214,9 @@
         for q in range(4):
             spread(
                 xt.at[p, :, pl.ds(768 * q, 768)],
-                pt.at[c // 4, p, slice16, :],
+                pt.at[j, p, slice16, :],
                 base_first + 4 * p,
-                (c // 4, 4 * r + q),
+                (j, 4 * r + q),
                 first_self & (c % 4 == q),
                 q,
                 1,
@@ -274,7 +274,7 @@
                 pt.at[r, p, pl.ds(16 * i, 16), :],
                 mate,
                 base_first + 4 * p + i,
-                first_self & (c % 4 == i),
+                first_self & (zh == i),
             )
         got_z, got_yp, got_yn = to(zmate, r), to(yn, r), to(yp, r)
         to_mate(r)
@@ -303,12 +303,16 @@
             links.arrived(ptx.at[row, p], mate, slot)
         yield
 
+    def in_order(ref, p, h):
+        return jnp.concatenate(
+            [ref[k, p, pl.ds(16 * i, 16)] for i in (2 * h, 2 * h + 1) for k in range(8)], axis=0
+        )
+
     def product(p, xx, out):
         left = ao[:, xx].reshape(NZH * SHARE, BLOCK)
         left_x = ax[:, xx].reshape(NZH * SHARE, BLOCK)
         for h in range(2):
-            right = pt[pl.ds(4 * h, 4), p].reshape(256, BLOCK)
-            right_x = ptx[pl.ds(4 * h, 4), p].reshape(256, BLOCK)
+            right, right_x = in_order(pt, p, h), in_order(ptx, p, h)
             value = nt_dot(left, right) + nt_dot(left_x, right_x)
             out[..., pl.ds(256 * h, 256)] = value.reshape(NZH, SHARE, 256).astype(out.dtype)
 
@@ -497,9 +501,11 @@
     def assemble(out, source, first, pivot):
         for k in range(8):
             for d in range(NY):
-                rows, cols = slice(64 * k, 64 * k + 64), slice(128 * d, 128 * d + 128)
-                part = source[k, d, first : first + 64].astype(F32)
-                out[rows, cols] = part if pivot is None else pivot[rows, cols] - part
+                for i in range(4):
+                    start = 16 * (8 * i + k)
+                    rows, cols = slice(start, start + 16), slice(128 * d, 128 * d + 128)
+                    part = source[k, d, first + 16 * i : first + 16 * i + 16].astype(F32)
+                    out[rows, cols] = part if pivot is None else pivot[rows, cols] - part
 
     def parts_dot(dot, wide):
         high = wide.astype(BF16)

time: 120 us -> 128 us (1.067)
  Pallas kernels: 119 us -> 127 us
    pallas_call x1, Pallas kernels: 116 us -> 125 us  [body(): pl.pallas_call(kernel, out_shape=(jax.ShapeDtypeStruct((SHARE, W), BF16),...]
where the time goes in v6:
time: 128 us
  Pallas kernels  127 us (99%)
    pallas_call x1, Pallas kernels, body(): pl.pallas_call(kernel, out_shape=(jax.ShapeDtypeStruct((SHARE, W), BF16),...  125 us

profile of v6, /device:TPU:1, one launch (start us, length us, event | category | flops | bytes accessed | tf_op | source)
XLA Modules:
  0.0 128.1 jit_solution(16351226459661497944)
XLA Ops:
  0.6 0.0 copy-start
  0.6 0.0 copy-start.2
  0.7 0.0 copy-start.1
  0.7 124.9 %shard_map.128 = (bf16[96,512]{1,0:T(8,128)(2,1)S(1)}, bf16[96,512]{1,0:T(8,128)(2,1)S(1)}, bf16[8,4,128,128]{3,2,1,0:T(8,128)(2,1)S(1)}, bf16[8,4,64,128]{3,2,1,0:T(8,128)(2,1)S(1)}) custom-call(bf16[4,4,2,96,768]{4,3,2,1,0:T(8,128)(2,1)} %bitcast.5, s32[64,64]{1,0:T(8,128)} %pattern_ref.1, bf16[16,3072]{1,0:T(8,128)(2,1)} %bitcast.6, ...), custom_call_target="tpu_custom_call" | custom-call | tf_op jit(solution)/shard_map/pallas_call | solution.py:555
  125.6 0.0 copy-done
  125.6 0.0 copy-done.2
  125.6 0.0 copy-done.1
  125.6 2.5 %shard_map.129 = (f32[512,512]{1,0:T(8,128)}, f32[512,512]{1,0:T(8,128)}, f32[512,512]{1,0:T(8,128)}, bf16[96,512]{1,0:T(8,128)(2,1)}, bf16[96,512]{1,0:T(8,128)(2,1)}) custom-call(bf16[512,512]{1,0:T(8,128)(2,1)S(1)} %copy-done, f32[512,512]{1,0:T(8,128)S(1)} %copy-done.1, f32[512,512]{1,0:T(8,128)S(1)} %copy-done.2, ...), custom_call_target="tpu_custom_call" | custom-call | tf_op jit(solution)/shard_map/pallas_call | solution.py:613
Async XLA Ops:
  0.6 124.9 %copy-start = (bf16[512,512]{1,0:T(8,128)(2,1)S(1)}, bf16[512,512]{1,0:T(8,128)(2,1)}, u32[]{:S(2)}) copy-start(bf16[512,512]{1,0:T(8,128)(2,1)} %inner_ref.3) | copy-start | bytes 1572868
  0.6 124.9 %copy-start.2 = (f32[512,512]{1,0:T(8,128)S(1)}, f32[512,512]{1,0:T(8,128)}, u32[]{:S(2)}) copy-start(f32[512,512]{1,0:T(8,128)} %pivot2_ref.1) | copy-start | bytes 3145732
  0.7 124.9 %copy-start.1 = (f32[512,512]{1,0:T(8,128)S(1)}, f32[512,512]{1,0:T(8,128)}, u32[]{:S(2)}) copy-start(f32[512,512]{1,0:T(8,128)} %pivot1_ref.1) | copy-start | bytes 3145732

commit v7 on v5

--- a/solution.py
+++ b/solution.py
@@ -138,8 +138,9 @@
         return (y + e // 8) % NY, (z + e % 8) % 8
 
     barrier = pltpu.get_barrier_semaphore()
-    first_self = c // 4 == r
-    own_self = (c // 4 == r) & (8 * (c % 4) + r == c)
+    held = zl * NY + (y + 8 - c // 4) % NY
+    first_self = (c // 4 == r) & (held == r)
+    own_self = (c // 4 == r) & (8 * (c % 4) + held == c)
     for device in [mate, xn, xp]:
         pl.semaphore_signal(barrier, inc=1, device_id=device, device_id_type=MESH)
 
@@ -155,11 +156,11 @@
 
         @pl.when(jnp.logical_not(first_self & (c % 4 == i)))
         def _():
-            pl.semaphore_signal(barrier, inc=1, device_id=(c // 4, 4 * r + i), device_id_type=MESH)
+            pl.semaphore_signal(barrier, inc=1, device_id=(c // 4, 4 * held + i), device_id_type=MESH)
 
     @pl.when(jnp.logical_not(own_self))
     def _():
-        pl.semaphore_signal(barrier, inc=1, device_id=(j, 4 * r + zh), device_id_type=MESH)
+        pl.semaphore_signal(barrier, inc=1, device_id=(j // 4 * NY + (j + r) % NY, 4 * r + zh), device_id_type=MESH)
 
     own_rows = pl.ds(pl.multiple_of(24 * r, 8), 24)
     loads = [
@@ -216,7 +217,7 @@
                 xt.at[p, :, pl.ds(768 * q, 768)],
                 pt.at[c // 4, p, slice16, :],
                 base_first + 4 * p,
-                (c // 4, 4 * r + q),
+                (c // 16 * NY + (c // 4 + r) % NY, 4 * r + q),
                 first_self & (c % 4 == q),
                 q,
                 1,
@@ -227,11 +228,11 @@
     a_slot = links.send(a_ref.at[:, :, 1 - core], ax, mate)
 
     def send_own_rows():
-        links.send(pt.at[r], mx, (c // 4, 8 * (c % 4) + r), own_slot, own_self)
+        links.send(pt.at[held], mx, (c // 4, 8 * (c % 4) + held), own_slot, own_self)
 
         @pl.when(own_self)
         def _():
-            local = pltpu.make_async_copy(pt.at[r], mx, local_sem.at[2])
+            local = pltpu.make_async_copy(pt.at[held], mx, local_sem.at[2])
             local.start()
             local.wait()
 
@@ -252,7 +253,7 @@
     mask_rows(ao, c)
 
     def row_of(yy, zz):
-        return zz * NY + yy
+        return zz * NY + (yy + 8 - c // 4) % NY
 
     r_z = row_of(y, 1 - zl)
     y_p, y_n, y_d = (y + 3) % NY, (y + 1) % NY, (y + 2) % NY
@@ -271,13 +272,13 @@
 
         for i in range(4):
             links.arrived(
-                pt.at[r, p, pl.ds(16 * i, 16), :],
+                pt.at[held, p, pl.ds(16 * i, 16), :],
                 mate,
                 base_first + 4 * p + i,
                 first_self & (c % 4 == i),
             )
-        got_z, got_yp, got_yn = to(zmate, r), to(yn, r), to(yp, r)
-        to_mate(r)
+        got_z, got_yp, got_yn = to(zmate, held), to(yn, held), to(yp, held)
+        to_mate(held)
         yield
         links.arrived(pt.at[r_z, p], zmate, got_z)
         got_yp_z, got_yn_z = to(yn, r_z), to(yp, r_z)

time: 120 us -> 120 us (level)
  no operation moved by 1% of the time
where the time goes in v7:
time: 120 us; the launch traced here: 119 us
  Pallas kernels  119 us (99%)
    pallas_call x1, Pallas kernels, body(): pl.pallas_call(kernel, out_shape=(jax.ShapeDtypeStruct((SHARE, W), BF16),...  116 us
    pallas_call x1, Pallas kernels, body(): pl.pallas_call(finish, out_shape=(wide, wide, wide, narrow, narrow), in_s...  2.49 us

profile of v7, /device:TPU:1, one launch (start us, length us, event | category | flops | bytes accessed | tf_op | source)
XLA Modules:
  0.0 119.5 jit_solution(18344613945602322768)
XLA Ops:
  0.6 0.0 copy-start
  0.6 0.0 copy-start.2
  0.7 0.0 copy-start.1
  0.7 116.3 %shard_map.128 = (bf16[96,512]{1,0:T(8,128)(2,1)S(1)}, bf16[96,512]{1,0:T(8,128)(2,1)S(1)}, bf16[8,4,128,128]{3,2,1,0:T(8,128)(2,1)S(1)}, bf16[8,4,64,128]{3,2,1,0:T(8,128)(2,1)S(1)}) custom-call(bf16[4,4,2,96,768]{4,3,2,1,0:T(8,128)(2,1)} %bitcast.5, s32[64,64]{1,0:T(8,128)} %pattern_ref.1, bf16[16,3072]{1,0:T(8,128)(2,1)} %bitcast.6, ...), custom_call_target="tpu_custom_call" | custom-call | tf_op jit(solution)/shard_map/pallas_call | solution.py:550
  116.9 0.0 copy-done
  117.0 0.0 copy-done.2
  117.0 0.0 copy-done.1
  117.0 2.5 %shard_map.129 = (f32[512,512]{1,0:T(8,128)}, f32[512,512]{1,0:T(8,128)}, f32[512,512]{1,0:T(8,128)}, bf16[96,512]{1,0:T(8,128)(2,1)}, bf16[96,512]{1,0:T(8,128)(2,1)}) custom-call(bf16[512,512]{1,0:T(8,128)(2,1)S(1)} %copy-done, f32[512,512]{1,0:T(8,128)S(1)} %copy-done.1, f32[512,512]{1,0:T(8,128)S(1)} %copy-done.2, ...), custom_call_target="tpu_custom_call" | custom-call | tf_op jit(solution)/shard_map/pallas_call | solution.py:608
Async XLA Ops:
  0.6 116.3 %copy-start = (bf16[512,512]{1,0:T(8,128)(2,1)S(1)}, bf16[512,512]{1,0:T(8,128)(2,1)}, u32[]{:S(2)}) copy-start(bf16[512,512]{1,0:T(8,128)(2,1)} %inner_ref.3) | copy-start | bytes 1572868
  0.6 116.3 %copy-start.2 = (f32[512,512]{1,0:T(8,128)S(1)}, f32[512,512]{1,0:T(8,128)}, u32[]{:S(2)}) copy-start(f32[512,512]{1,0:T(8,128)} %pivot2_ref.1) | copy-start | bytes 3145732
  0.7 116.3 %copy-start.1 = (f32[512,512]{1,0:T(8,128)S(1)}, f32[512,512]{1,0:T(8,128)}, u32[]{:S(2)}) copy-start(f32[512,512]{1,0:T(8,128)} %pivot1_ref.1) | copy-start | bytes 3145732
